TPU v7x, 128 devices: a whole 4x4x4 slice. The times are simulated.
128 devices in a mesh: sta: 16 (over z, y), tile: 8 (over x, core).
Axes of the slice: x: 4, y: 4, z: 4, core: 2. Of those that a mesh axis runs over, the one named last changes fastest.
Arguments:
- traces: bfloat16 [3072, 3072], P('sta', 'tile'), may hold values from -6 to 6
- fir_taps: float32 [4, 64], replicated, may hold values from -0.75 to 0.75
- band_gain: float32 [4], replicated, may hold values from 0.5 to 2
- starts: int32 [3072, 8], P('sta'), may hold values from 0 to 2688
- delays: int32 [3072, 16384], P('sta', 'tile'), may hold values from 0 to 127
- visibility: int32 [3072, 8], P('sta'), may hold values from 0 to 1, as said below
Outputs:
- image: float32 [16384, 256], P(('tile', 'sta'))
Inputs may be any that keep to these rules, and one draw needn't show every extreme that they name: `visibility`: 1 where the station contributes to the tile's grid points, else 0; how many stations a tile uses may differ from tile to tile.
All inputs are finite; a program needn't handle non-finite values.
Results may differ from a plain program's by a relative error of at most 0.0051.
Values may be sent and summed in bfloat16 or wider, within the bound.
No kernel may reach another device: no remote copies, remote signals or barrier semaphores. Data moves between devices by JAX's collectives and lax.ppermute only.
A program may use at most 64 MiB of HBM per device.

v0:
```python
import functools
import math

import jax
import jax.numpy as jnp
from jax import lax
from jax.experimental import pallas as pl
from jax.experimental.pallas import tpu as pltpu
from jax.sharding import Mesh, PartitionSpec as P

TAPS = 64
D = 128
L = 256
WLEN = 384
BANDS = 4
LANE = 128
BF16 = jnp.bfloat16
F32 = jnp.float32
VMEM_LIMIT = 60 << 20


def vmem():
    return pl.BlockSpec(memory_space=pltpu.VMEM)


def smem():
    return pl.BlockSpec(memory_space=pltpu.SMEM)


def shift_to(value, axis, by):
    length = lax.axis_size(axis)
    return lax.ppermute(value, axis, [(i, (i + by) % length) for i in range(length)])


def prep_kernel(place, delays, taps, *outs):
    pieces, toeplitz = outs[:-1], outs[-1]
    z = place[0]
    stations, width = delays.shape[0], delays.shape[1] // len(pieces)
    for k, piece in enumerate(pieces):
        chunk = lax.rem(z + k, len(pieces))
        rows = delays[:, pl.ds(pl.multiple_of(chunk * width, LANE), width)].astype(F32)
        columns = jnp.transpose(rows)
        tail = columns[:, LANE:stations]
        piece[:, 0:LANE] = columns[:, 0:LANE].astype(BF16)
        piece[:, LANE : 2 * LANE] = jnp.concatenate([tail, tail - 1.0], axis=1).astype(BF16)
    for b in range(BANDS):
        row = jnp.broadcast_to(taps[b : b + 1, :], (2 * LANE, 2 * LANE))
        band = pltpu.roll(row, 0, axis=1, stride=1, stride_axis=0)[:, 0:LANE]
        for part in range(3):
            rounded = band.astype(BF16)
            toeplitz[part, :, b * LANE : (b + 1) * LANE] = rounded
            band = band - rounded.astype(F32)


def window_kernel(place, gain, mine, other, starts, visibility, toeplitz, out, line):
    x, core = place[2], place[3]
    stations, samp = mine.shape[1], mine.shape[2]
    chips = mine.shape[0]
    tiles_in = (2 * chips * samp) // LANE
    line[:, 0:LANE] = jnp.zeros((stations, LANE), F32)
    line[:, (tiles_in + 1) * LANE :] = jnp.zeros((stations, LANE), F32)
    for k in range(chips):
        chip = lax.rem(x + chips - k, chips)
        for src, c in ((mine, core), (other, 1 - core)):
            at = pl.multiple_of((2 * chip + c) * samp + LANE, LANE)
            line[:, pl.ds(at, samp)] = src[k].astype(F32)
    tile = 2 * x + core
    lane = lax.broadcasted_iota(jnp.int32, starts.shape, 1)
    first = jnp.sum(jnp.where(lane == tile, starts[...], 0), axis=1, keepdims=True) + (LANE - TAPS + 1)
    visible = jnp.sum(jnp.where(lane == tile, visibility[...], 0), axis=1, keepdims=True).astype(F32)
    parts = [line[:, i * LANE : (i + 1) * LANE] for i in range(tiles_in + 2)]
    keep = WLEN // LANE + 2
    bit = 16
    while bit:
        size = min(len(parts), bit - 1 + keep)
        chosen = (first & (bit * LANE)) != 0
        parts = [
            jnp.where(chosen, parts[i + bit], parts[i]) if i + bit < len(parts) else parts[i]
            for i in range(size)
        ]
        bit //= 2
    span = jnp.concatenate(parts, axis=1)
    width = span.shape[1]
    bit = LANE // 2
    while bit:
        chosen = (first & bit) != 0
        span = jnp.where(chosen, pltpu.roll(span, width - bit, axis=1), span)
        bit //= 2
    span = span.astype(BF16)
    blocks = jnp.concatenate([span[:, j * LANE : j * LANE + 2 * LANE] for j in range(WLEN // LANE)], axis=0)
    filtered = sum(jnp.dot(blocks, toeplitz[p], preferred_element_type=F32) for p in range(3))
    char = sum(gain[b] * jnp.square(filtered[:, b * LANE : (b + 1) * LANE]) for b in range(BANDS))
    char = char.astype(BF16).astype(F32)
    char = jnp.concatenate([char[j * stations : (j + 1) * stations] for j in range(WLEN // LANE)], axis=1)
    mean = jnp.sum(char, axis=1, keepdims=True) / WLEN
    out[...] = ((char - mean) * visible).astype(BF16)


def one_hot(column, level):
    return jnp.where(column == jnp.asarray(level, BF16), jnp.asarray(1, BF16), jnp.asarray(0, BF16))


def stack_parts(columns, windows, table):
    w = windows[...]
    for d in range(D):
        rolled = pltpu.roll(w, (WLEN - d) % WLEN, axis=1)[:, 0:L]
        table[d * LANE : (d + 1) * LANE, :] = rolled[0:LANE]
        half = LANE // 2
        table[D * LANE + d * half : D * LANE + (d + 1) * half, :] = rolled[LANE:]
    head, tail = columns[:, 0:LANE], columns[:, LANE : 2 * LANE]
    picks = [one_hot(head, d) for d in range(D)] + [one_hot(tail, d) for d in range(0, D, 2)]
    return jnp.dot(jnp.concatenate(picks, axis=1), table[...], preferred_element_type=F32)


def own_kernel(columns, windows, out, table):
    out[...] = stack_parts(columns, windows, table)


def rest_kernel(place, acc, *refs):
    count = 3
    columns, windows = refs[:count], refs[count : 2 * count]
    kept, sends = refs[2 * count], refs[2 * count + 1 : 2 * count + 4]
    table, total, now_columns, now_windows = refs[2 * count + 4 :]
    step = pl.program_id(0)
    for k in range(count):

        @pl.when(step == k)
        def _():
            now_columns[...] = columns[k][...]
            now_windows[...] = windows[k][...]

    @pl.when(step == 0)
    def _():
        total[...] = acc[...]

    total[...] += stack_parts(now_columns, now_windows, table)

    @pl.when(step == count - 1)
    def _():
        y = place[1]
        rows = kept.shape[0]
        kept[...] = total[pl.ds(pl.multiple_of(y * rows, rows), rows), :]
        for k, send in enumerate(sends):
            at = lax.rem(y + k + 1, 4)
            send[...] = total[pl.ds(pl.multiple_of(at * rows, rows), rows), :].astype(BF16)


def on_device(traces, fir_taps, band_gain, starts, delays, visibility):
    stations, samp = traces.shape
    grid_dev = delays.shape[1]
    piece = grid_dev // 4
    place = jnp.stack([lax.axis_index(a) for a in ("z", "y", "x", "core")]).astype(jnp.int32)
    params = pltpu.CompilerParams(vmem_limit_bytes=VMEM_LIMIT)

    near = [traces] + [shift_to(traces, "x", k) for k in (1, 2, 3)]

    circle = jnp.concatenate(
        [fir_taps[:, TAPS - 1 :], jnp.zeros((BANDS, 2 * LANE - TAPS), F32), fir_taps[:, : TAPS - 1]], axis=1
    )
    prepared = pl.pallas_call(
        prep_kernel,
        out_shape=[jax.ShapeDtypeStruct((piece, 2 * LANE), BF16)] * 4
        + [jax.ShapeDtypeStruct((3, 2 * LANE, BANDS * LANE), BF16)],
        in_specs=[smem(), vmem(), vmem()],
        out_specs=[vmem()] * 5,
        compiler_params=params,
        name="prep",
    )(place, delays, circle)
    own_columns, toeplitz = prepared[0], prepared[4]
    far_columns = [shift_to(prepared[k], "z", k) for k in (1, 2, 3)]

    mine = jnp.stack(near)
    other = shift_to(mine, "core", 1)
    windows = pl.pallas_call(
        window_kernel,
        out_shape=jax.ShapeDtypeStruct((stations, WLEN), BF16),
        in_specs=[smem(), smem()] + [vmem()] * 5,
        out_specs=vmem(),
        scratch_shapes=[pltpu.VMEM((stations, 8 * samp + 2 * LANE), F32)],
        compiler_params=params,
        name="window",
    )(place, band_gain, mine, other, starts, visibility, toeplitz)
    far_windows = [shift_to(windows, "z", k) for k in (1, 2, 3)]

    table = pltpu.VMEM((stations * D, L), BF16)
    flops = 2 * piece * stations * D * L
    own = pl.pallas_call(
        own_kernel,
        out_shape=jax.ShapeDtypeStruct((piece, L), F32),
        in_specs=[vmem()] * 2,
        out_specs=vmem(),
        scratch_shapes=[table],
        compiler_params=params,
        cost_estimate=pl.CostEstimate(flops=flops, bytes_accessed=1 << 20, transcendentals=0),
        name="own",
    )(own_columns, windows)
    rows = piece // 4
    kept, *sends = pl.pallas_call(
        rest_kernel,
        grid=(3,),
        out_shape=[jax.ShapeDtypeStruct((rows, L), F32)] + [jax.ShapeDtypeStruct((rows, L), BF16)] * 3,
        in_specs=[smem()] + [vmem()] * 7,
        out_specs=[vmem()] * 4,
        scratch_shapes=[
            table,
            pltpu.VMEM((piece, L), F32),
            pltpu.VMEM((piece, 2 * LANE), BF16),
            pltpu.VMEM((stations, WLEN), BF16),
        ],
        compiler_params=params,
        cost_estimate=pl.CostEstimate(flops=3 * flops, bytes_accessed=2 << 20, transcendentals=0),
        name="rest",
    )(place, own, *far_columns, *far_windows)
    received = [shift_to(send, "y", k + 1) for k, send in enumerate(sends)]
    total = kept + sum(r.astype(F32) for r in received)
    return total / math.sqrt(stations * 16)


def solution(mesh):
    split = Mesh(mesh.devices.reshape(4, 4, 4, 2), ("z", "y", "x", "core"))
    sta, tile = ("z", "y"), ("x", "core")
    placed = (P(sta, tile), P(), P(), P(sta, None), P(sta, tile), P(sta, None))
    return jax.shard_map(
        on_device, mesh=split, in_specs=placed, out_specs=P(("x", "core", "z", "y"), None), check_vma=False
    )
```

profile of v0, /device:TPU:6, one launch (start us, length us, event | category | flops | bytes accessed | tf_op | source)
XLA Modules:
  0.0 76.1 jit_solution(14904611726228600154)
XLA Ops:
  0.0 0.4 collective-permute-start
  0.4 1.6 %collective-permute-start.2 = (bf16[192,384]{1,0:T(8,128)(2,1)}, bf16[192,384]{1,0:T(8,128)(2,1)S(1)}, u32[]{:S(2)}, u32[]{:S(2)}) collective-permute-start(bf16[192,384]{1,0:T(8,128)(2,1)} %param.6), channel_id=1, source_target_pairs={{0,6},{2,0},{4,2},{6,4},{1,7},{3,1},{5,3},{7,5},{8,14},{10,8},{12,... | collective-permute-start | bytes 442376 | tf_op jit(solution)/shard_map/ppermute | solution.py:32
  2.0 1.4 %collective-permute-start.1 = (bf16[192,384]{1,0:T(8,128)(2,1)}, bf16[192,384]{1,0:T(8,128)(2,1)S(1)}, u32[]{:S(2)}, u32[]{:S(2)}) collective-permute-start(bf16[192,384]{1,0:T(8,128)(2,1)} %param.6), channel_id=1, source_target_pairs={{0,4},{2,6},{4,0},{6,2},{1,5},{3,7},{5,1},{7,3},{8,12},{10,14},{12... | collective-permute-start | bytes 442376 | tf_op jit(solution)/shard_map/ppermute | solution.py:32
  3.4 0.8 slice.6
  4.2 0.1 pad.5.clone
  4.3 2.7 %collective-permute-done = bf16[192,384]{1,0:T(8,128)(2,1)S(1)} collective-permute-done((bf16[192,384]{1,0:T(8,128)(2,1)}, bf16[192,384]{1,0:T(8,128)(2,1)S(1)}, u32[]{:S(2)}, u32[]{:S(2)}) %collective-permute-start) | collective-permute-done | bytes 147488 | tf_op jit(solution)/shard_map/ppermute | solution.py:32
  7.0 3.3 %collective-permute-done.2 = bf16[192,384]{1,0:T(8,128)(2,1)S(1)} collective-permute-done((bf16[192,384]{1,0:T(8,128)(2,1)}, bf16[192,384]{1,0:T(8,128)(2,1)S(1)}, u32[]{:S(2)}, u32[]{:S(2)}) %collective-permute-start.2) | collective-permute-done | bytes 147488 | tf_op jit(solution)/shard_map/ppermute | solution.py:32
  10.3 0.0 collective-permute-done.1
  10.3 1.0 %pad_maximum_fusion.mine = bf16[4,192,384]{2,1,0:T(8,128)(2,1)S(1)} fusion(bf16[1,192,384]{2,1,0:T(8,128)(2,1)S(1)} %bitcast.11, bf16[1,192,384]{2,1,0:T(8,128)(2,1)S(1)} %bitcast.12, bf16[1,192,384]{2,1,0:T(8,128)(2,1)S(1)} %bitcast.10, bf16[1,192,384]{2,1,0:T(8,128)(2,1)} %bitcast.9), kind=kLoop, calls=%fused_computation | loop fusion | flops 884736 | bytes 1179648 | tf_op jit(solution)/shard_map/stack | solution.py:172
  11.3 0.1 collective-permute-start.3
  11.4 0.6 pad_add_fusion.place
  12.0 1.3 %pad_maximum_fusion.1.taps = f32[4,256]{1,0:T(4,128)} fusion(f32[4,63]{1,0:T(4,128)} %bitcast.13, f32[4,1]{1,0:T(4,128)S(1)} %slice.6, f32[256]{0:T(256)S(1)} %pad.5.clone), kind=kLoop, calls=%fused_computation.2 | loop fusion | flops 2048 | bytes 6144 | tf_op jit(solution)/shard_map/concatenate | solution.py:157
  13.4 3.2 %prep.1 = (bf16[512,256]{1,0:T(8,128)(2,1)}, bf16[512,256]{1,0:T(8,128)(2,1)}, bf16[512,256]{1,0:T(8,128)(2,1)}, bf16[512,256]{1,0:T(8,128)(2,1)}, bf16[3,256,512]{2,1,0:T(8,128)(2,1)}) custom-call(s32[4]{0:T(128)} %pad_add_fusion.place, s32[192,2048]{1,0:T(8,128)} %delays.1, f32[4,256]{1,0:T(4,128)} %pad_maximum_fusion.1.taps), custom_call_target="tpu_custom_call" | custom-call | tf_op jit(solution)/shard_map/prep/pallas_call | solution.py:160
  16.6 2.0 %collective-permute-start.4 = (bf16[512,256]{1,0:T(8,128)(2,1)}, bf16[512,256]{1,0:T(8,128)(2,1)S(1)}, u32[]{:S(2)}, u32[]{:S(2)}) collective-permute-start(bf16[512,256]{1,0:T(8,128)(2,1)} %get-tuple-element.16), channel_id=1, source_target_pairs={{0,32},{32,64},{64,96},{96,0},{1,33},{33,65},{65,97},{97,1},{2,34}... | collective-permute-start | bytes 786440 | tf_op jit(solution)/shard_map/ppermute | solution.py:32
  18.6 3.6 %collective-permute-start.5 = (bf16[512,256]{1,0:T(8,128)(2,1)}, bf16[512,256]{1,0:T(8,128)(2,1)S(1)}, u32[]{:S(2)}, u32[]{:S(2)}) collective-permute-start(bf16[512,256]{1,0:T(8,128)(2,1)} %get-tuple-element.17), channel_id=1, source_target_pairs={{0,64},{32,96},{64,0},{96,32},{1,65},{33,97},{65,1},{97,33},{2,66}... | collective-permute-start | bytes 786440 | tf_op jit(solution)/shard_map/ppermute | solution.py:32
  22.2 1.0 %collective-permute-start.6 = (bf16[512,256]{1,0:T(8,128)(2,1)}, bf16[512,256]{1,0:T(8,128)(2,1)S(1)}, u32[]{:S(2)}, u32[]{:S(2)}) collective-permute-start(bf16[512,256]{1,0:T(8,128)(2,1)} %get-tuple-element.18), channel_id=1, source_target_pairs={{0,96},{32,0},{64,32},{96,64},{1,97},{33,1},{65,33},{97,65},{2,98}... | collective-permute-start | bytes 786440 | tf_op jit(solution)/shard_map/ppermute | solution.py:32
  23.2 0.0 copy-done.2
  23.2 0.8 copy.7.starts
  24.0 0.0 copy-done.3
  24.0 0.8 copy.8.visibility
  24.7 0.0 collective-permute-done.3.other
  24.7 0.0 copy-done
  24.7 0.8 %copy-done.1 = bf16[4,192,384]{2,1,0:T(8,128)(2,1)} copy-done((bf16[4,192,384]{2,1,0:T(8,128)(2,1)}, bf16[4,192,384]{2,1,0:T(8,128)(2,1)S(1)}, u32[]{:S(2)}) %copy-start.1) | copy-done | bytes 589848
  25.6 3.9 %window.1.windows = bf16[192,384]{1,0:T(8,128)(2,1)} custom-call(s32[4]{0:T(128)} %pad_add_fusion.place, f32[4]{0:T(128)} %gain.1, bf16[4,192,384]{2,1,0:T(8,128)(2,1)} %copy-done, bf16[4,192,384]{2,1,0:T(8,128)(2,1)} %copy-done.1, s32[192,8]{1,0:T(8,128)} %copy.7.starts, s32[192,8]{1,0:T(8,128)} %copy.8.visibility, ...), custom_call_target="tpu_custom_call" | custom-call | tf_op jit(solution)/shard_map/window/pallas_call | solution.py:174
  29.5 0.0 collective-permute-start.9
  29.5 3.1 %collective-permute-start.8 = (bf16[192,384]{1,0:T(8,128)(2,1)}, bf16[192,384]{1,0:T(8,128)(2,1)S(1)}, u32[]{:S(2)}, u32[]{:S(2)}) collective-permute-start(bf16[192,384]{1,0:T(8,128)(2,1)} %window.1.windows), channel_id=1, source_target_pairs={{0,64},{32,96},{64,0},{96,32},{1,65},{33,97},{65,1},{97,33},{2,66}... | collective-permute-start | bytes 442376 | tf_op jit(solution)/shard_map/ppermute | solution.py:32
  32.6 0.0 collective-permute-done.4.refs_0_
  32.6 0.1 collective-permute-start.7
  32.7 8.6 %own.1.acc = f32[512,256]{1,0:T(8,128)} custom-call(bf16[512,256]{1,0:T(8,128)(2,1)} %get-tuple-element.14.columns, bf16[192,384]{1,0:T(8,128)(2,1)} %window.1.windows), custom_call_target="tpu_custom_call" | custom-call | flops 6442450944 | bytes 1048576 | tf_op jit(solution)/shard_map/own/pallas_call | solution.py:187
  41.3 0.0 collective-permute-done.5.refs_1_
  41.3 0.0 collective-permute-done.6.refs_2_
  41.3 0.0 collective-permute-done.9.refs_5_
  41.3 0.0 collective-permute-done.8.refs_4_
  41.3 0.0 copy-start.8
  41.3 0.0 collective-permute-done.7.refs_3_
  41.3 0.6 copy-done.5
  42.0 0.1 copy-done.6
  42.1 0.1 copy-done.7
  42.1 0.1 copy-done.8
  42.2 0.7 copy-done.9
  42.9 22.7 %rest.1 = (f32[128,256]{1,0:T(8,128)}, bf16[128,256]{1,0:T(8,128)(2,1)}, bf16[128,256]{1,0:T(8,128)(2,1)}, bf16[128,256]{1,0:T(8,128)(2,1)}) custom-call(s32[4]{0:T(128)} %pad_add_fusion.place, f32[512,256]{1,0:T(8,128)} %own.1.acc, bf16[512,256]{1,0:T(8,128)(2,1)} %copy-done.4, bf16[512,256]{1,0:T(8,128)(2,1)} %copy-done.5, bf16[512,256]{1,0:T(8,128)(2,1)} %copy-done.6, ...), custom_call_target="tpu_custom_call" | custom-call | flops 19327352832 | bytes 2097152 | tf_op jit(solution)/shard_map/rest/pallas_call | solution.py:198
  65.6 1.6 %collective-permute-start.10 = (bf16[128,256]{1,0:T(8,128)(2,1)}, bf16[128,256]{1,0:T(8,128)(2,1)S(1)}, u32[]{:S(2)}, u32[]{:S(2)}) collective-permute-start(bf16[128,256]{1,0:T(8,128)(2,1)} %get-tuple-element.20), channel_id=1, source_target_pairs={{0,8},{8,16},{16,24},{24,0},{1,9},{9,17},{17,25},{25,1},{2,10},{10... | collective-permute-start | bytes 196616 | tf_op jit(solution)/shard_map/ppermute | solution.py:32
  67.1 2.9 %collective-permute-start.11 = (bf16[128,256]{1,0:T(8,128)(2,1)}, bf16[128,256]{1,0:T(8,128)(2,1)S(1)}, u32[]{:S(2)}, u32[]{:S(2)}) collective-permute-start(bf16[128,256]{1,0:T(8,128)(2,1)} %get-tuple-element.21), channel_id=1, source_target_pairs={{0,16},{8,24},{16,0},{24,8},{1,17},{9,25},{17,1},{25,9},{2,18},{10... | collective-permute-start | bytes 196616 | tf_op jit(solution)/shard_map/ppermute | solution.py:32
  70.0 1.3 %collective-permute-start.12 = (bf16[128,256]{1,0:T(8,128)(2,1)}, bf16[128,256]{1,0:T(8,128)(2,1)S(1)}, u32[]{:S(2)}, u32[]{:S(2)}) collective-permute-start(bf16[128,256]{1,0:T(8,128)(2,1)} %get-tuple-element.22), channel_id=1, source_target_pairs={{0,24},{8,0},{16,8},{24,16},{1,25},{9,1},{17,9},{25,17},{2,26},{10... | collective-permute-start | bytes 196616 | tf_op jit(solution)/shard_map/ppermute | solution.py:32
  71.4 0.6 collective-permute-done.10
  72.0 1.2 %collective-permute-done.11 = bf16[128,256]{1,0:T(8,128)(2,1)S(1)} collective-permute-done((bf16[128,256]{1,0:T(8,128)(2,1)}, bf16[128,256]{1,0:T(8,128)(2,1)S(1)}, u32[]{:S(2)}, u32[]{:S(2)}) %collective-permute-start.11) | collective-permute-done | bytes 65568 | tf_op jit(solution)/shard_map/ppermute | solution.py:32
  73.2 1.3 %collective-permute-done.12 = bf16[128,256]{1,0:T(8,128)(2,1)S(1)} collective-permute-done((bf16[128,256]{1,0:T(8,128)(2,1)}, bf16[128,256]{1,0:T(8,128)(2,1)S(1)}, u32[]{:S(2)}, u32[]{:S(2)}) %collective-permute-start.12) | collective-permute-done | bytes 65568 | tf_op jit(solution)/shard_map/ppermute | solution.py:32
  74.5 1.6 %add_multiply_fusion = f32[128,256]{1,0:T(8,128)} fusion(f32[128,256]{1,0:T(8,128)} %get-tuple-element.19, bf16[128,256]{1,0:T(8,128)(2,1)S(1)} %collective-permute-done.12, bf16[128,256]{1,0:T(8,128)(2,1)S(1)} %collective-permute-done.11, bf16[128,256]{1,0:T(8,128)(2,1)S(1)} %collective-permute-done.10), kind=kLoop, calls=%fused_computation.1 | loop fusion | flops 229376 | bytes 458752 | tf_op jit(solution)/shard_map/div | solution.py:216
  (11 shorter events, 0.0 us)
Async XLA Ops:
  0.0 23.2 %copy-start.2 = (s32[192,8]{0,1:T(8,128)S(1)}, s32[192,8]{0,1:T(8,128)}, u32[]{:S(2)}) copy-start(s32[192,8]{0,1:T(8,128)} %param.9) | copy-start | bytes 18436
  0.0 24.0 %copy-start.3 = (s32[192,8]{0,1:T(8,128)S(1)}, s32[192,8]{0,1:T(8,128)}, u32[]{:S(2)}) copy-start(s32[192,8]{0,1:T(8,128)} %param.11) | copy-start | bytes 18436
  0.0 6.9 %collective-permute-start = (bf16[192,384]{1,0:T(8,128)(2,1)}, bf16[192,384]{1,0:T(8,128)(2,1)S(1)}, u32[]{:S(2)}, u32[]{:S(2)}) collective-permute-start(bf16[192,384]{1,0:T(8,128)(2,1)} %param.6), channel_id=1, source_target_pairs={{0,2},{2,4},{4,6},{6,0},{1,3},{3,5},{5,7},{7,1},{8,10},{10,12},{12... | collective-permute-start | bytes 442376 | tf_op jit(solution)/shard_map/ppermute | solution.py:32
  0.4 9.9 %collective-permute-start.2 = (bf16[192,384]{1,0:T(8,128)(2,1)}, bf16[192,384]{1,0:T(8,128)(2,1)S(1)}, u32[]{:S(2)}, u32[]{:S(2)}) collective-permute-start(bf16[192,384]{1,0:T(8,128)(2,1)} %param.6), channel_id=1, source_target_pairs={{0,6},{2,0},{4,2},{6,4},{1,7},{3,1},{5,3},{7,5},{8,14},{10,8},{12,... | collective-permute-start | bytes 442376 | tf_op jit(solution)/shard_map/ppermute | solution.py:32
  2.0 8.2 %collective-permute-start.1 = (bf16[192,384]{1,0:T(8,128)(2,1)}, bf16[192,384]{1,0:T(8,128)(2,1)S(1)}, u32[]{:S(2)}, u32[]{:S(2)}) collective-permute-start(bf16[192,384]{1,0:T(8,128)(2,1)} %param.6), channel_id=1, source_target_pairs={{0,4},{2,6},{4,0},{6,2},{1,5},{3,7},{5,1},{7,3},{8,12},{10,14},{12... | collective-permute-start | bytes 442376 | tf_op jit(solution)/shard_map/ppermute | solution.py:32
  11.3 13.5 %copy-start = (bf16[4,192,384]{2,1,0:T(8,128)(2,1)}, bf16[4,192,384]{2,1,0:T(8,128)(2,1)S(1)}, u32[]{:S(2)}) copy-start(bf16[4,192,384]{2,1,0:T(8,128)(2,1)S(1)} %pad_maximum_fusion.mine) | copy-start | bytes 1769476
  11.3 13.4 %collective-permute-start.3 = (bf16[4,192,384]{2,1,0:T(8,128)(2,1)S(1)}, bf16[4,192,384]{2,1,0:T(8,128)(2,1)S(1)}, u32[]{:S(2)}, u32[]{:S(2)}) collective-permute-start(bf16[4,192,384]{2,1,0:T(8,128)(2,1)S(1)} %pad_maximum_fusion.mine), channel_id=1, source_target_pairs={{0,1},{1,0},{2,3},{3,2},{4,5},{5,4},{6,7},{7,6},{8,9},{9,8},{10,11... | collective-permute-start | bytes 1769480 | tf_op jit(solution)/shard_map/ppermute | solution.py:32
  16.6 16.0 %collective-permute-start.4 = (bf16[512,256]{1,0:T(8,128)(2,1)}, bf16[512,256]{1,0:T(8,128)(2,1)S(1)}, u32[]{:S(2)}, u32[]{:S(2)}) collective-permute-start(bf16[512,256]{1,0:T(8,128)(2,1)} %get-tuple-element.16), channel_id=1, source_target_pairs={{0,32},{32,64},{64,96},{96,0},{1,33},{33,65},{65,97},{97,1},{2,34}... | collective-permute-start | bytes 786440 | tf_op jit(solution)/shard_map/ppermute | solution.py:32
  18.6 22.7 %collective-permute-start.5 = (bf16[512,256]{1,0:T(8,128)(2,1)}, bf16[512,256]{1,0:T(8,128)(2,1)S(1)}, u32[]{:S(2)}, u32[]{:S(2)}) collective-permute-start(bf16[512,256]{1,0:T(8,128)(2,1)} %get-tuple-element.17), channel_id=1, source_target_pairs={{0,64},{32,96},{64,0},{96,32},{1,65},{33,97},{65,1},{97,33},{2,66}... | collective-permute-start | bytes 786440 | tf_op jit(solution)/shard_map/ppermute | solution.py:32
  22.2 19.1 %collective-permute-start.6 = (bf16[512,256]{1,0:T(8,128)(2,1)}, bf16[512,256]{1,0:T(8,128)(2,1)S(1)}, u32[]{:S(2)}, u32[]{:S(2)}) collective-permute-start(bf16[512,256]{1,0:T(8,128)(2,1)} %get-tuple-element.18), channel_id=1, source_target_pairs={{0,96},{32,0},{64,32},{96,64},{1,97},{33,1},{65,33},{97,65},{2,98}... | collective-permute-start | bytes 786440 | tf_op jit(solution)/shard_map/ppermute | solution.py:32
  24.7 0.8 %copy-start.1 = (bf16[4,192,384]{2,1,0:T(8,128)(2,1)}, bf16[4,192,384]{2,1,0:T(8,128)(2,1)S(1)}, u32[]{:S(2)}) copy-start(bf16[4,192,384]{2,1,0:T(8,128)(2,1)S(1)} %collective-permute-done.3.other) | copy-start | bytes 1769476
  29.5 11.8 %collective-permute-start.9 = (bf16[192,384]{1,0:T(8,128)(2,1)}, bf16[192,384]{1,0:T(8,128)(2,1)S(1)}, u32[]{:S(2)}, u32[]{:S(2)}) collective-permute-start(bf16[192,384]{1,0:T(8,128)(2,1)} %window.1.windows), channel_id=1, source_target_pairs={{0,96},{32,0},{64,32},{96,64},{1,97},{33,1},{65,33},{97,65},{2,98}... | collective-permute-start | bytes 442376 | tf_op jit(solution)/shard_map/ppermute | solution.py:32
  29.5 11.8 %collective-permute-start.8 = (bf16[192,384]{1,0:T(8,128)(2,1)}, bf16[192,384]{1,0:T(8,128)(2,1)S(1)}, u32[]{:S(2)}, u32[]{:S(2)}) collective-permute-start(bf16[192,384]{1,0:T(8,128)(2,1)} %window.1.windows), channel_id=1, source_target_pairs={{0,64},{32,96},{64,0},{96,32},{1,65},{33,97},{65,1},{97,33},{2,66}... | collective-permute-start | bytes 442376 | tf_op jit(solution)/shard_map/ppermute | solution.py:32
  32.6 8.7 %copy-start.4 = (bf16[512,256]{1,0:T(8,128)(2,1)}, bf16[512,256]{1,0:T(8,128)(2,1)S(1)}, u32[]{:S(2)}) copy-start(bf16[512,256]{1,0:T(8,128)(2,1)S(1)} %collective-permute-done.4.refs_0_) | copy-start | bytes 786436
  32.6 8.7 %collective-permute-start.7 = (bf16[192,384]{1,0:T(8,128)(2,1)}, bf16[192,384]{1,0:T(8,128)(2,1)S(1)}, u32[]{:S(2)}, u32[]{:S(2)}) collective-permute-start(bf16[192,384]{1,0:T(8,128)(2,1)} %window.1.windows), channel_id=1, source_target_pairs={{0,32},{32,64},{64,96},{96,0},{1,33},{33,65},{65,97},{97,1},{2,34}... | collective-permute-start | bytes 442376 | tf_op jit(solution)/shard_map/ppermute | solution.py:32
  41.3 0.7 copy-start.5
  41.3 0.8 %copy-start.6 = (bf16[512,256]{1,0:T(8,128)(2,1)}, bf16[512,256]{1,0:T(8,128)(2,1)S(1)}, u32[]{:S(2)}) copy-start(bf16[512,256]{1,0:T(8,128)(2,1)S(1)} %collective-permute-done.6.refs_2_) | copy-start | bytes 786436
  41.3 0.8 %copy-start.7 = (bf16[192,384]{1,0:T(8,128)(2,1)}, bf16[192,384]{1,0:T(8,128)(2,1)S(1)}, u32[]{:S(2)}) copy-start(bf16[192,384]{1,0:T(8,128)(2,1)S(1)} %collective-permute-done.9.refs_5_) | copy-start | bytes 442372
  41.3 0.9 %copy-start.8 = (bf16[192,384]{1,0:T(8,128)(2,1)}, bf16[192,384]{1,0:T(8,128)(2,1)S(1)}, u32[]{:S(2)}) copy-start(bf16[192,384]{1,0:T(8,128)(2,1)S(1)} %collective-permute-done.8.refs_4_) | copy-start | bytes 442372
  42.2 0.7 copy-start.9
  65.6 6.4 %collective-permute-start.10 = (bf16[128,256]{1,0:T(8,128)(2,1)}, bf16[128,256]{1,0:T(8,128)(2,1)S(1)}, u32[]{:S(2)}, u32[]{:S(2)}) collective-permute-start(bf16[128,256]{1,0:T(8,128)(2,1)} %get-tuple-element.20), channel_id=1, source_target_pairs={{0,8},{8,16},{16,24},{24,0},{1,9},{9,17},{17,25},{25,1},{2,10},{10... | collective-permute-start | bytes 196616 | tf_op jit(solution)/shard_map/ppermute | solution.py:32
  67.1 6.1 %collective-permute-start.11 = (bf16[128,256]{1,0:T(8,128)(2,1)}, bf16[128,256]{1,0:T(8,128)(2,1)S(1)}, u32[]{:S(2)}, u32[]{:S(2)}) collective-permute-start(bf16[128,256]{1,0:T(8,128)(2,1)} %get-tuple-element.21), channel_id=1, source_target_pairs={{0,16},{8,24},{16,0},{24,8},{1,17},{9,25},{17,1},{25,9},{2,18},{10... | collective-permute-start | bytes 196616 | tf_op jit(solution)/shard_map/ppermute | solution.py:32
  70.0 4.5 %collective-permute-start.12 = (bf16[128,256]{1,0:T(8,128)(2,1)}, bf16[128,256]{1,0:T(8,128)(2,1)S(1)}, u32[]{:S(2)}, u32[]{:S(2)}) collective-permute-start(bf16[128,256]{1,0:T(8,128)(2,1)} %get-tuple-element.22), channel_id=1, source_target_pairs={{0,24},{8,0},{16,8},{24,16},{1,25},{9,1},{17,9},{25,17},{2,26},{10... | collective-permute-start | bytes 196616 | tf_op jit(solution)/shard_map/ppermute | solution.py:32
where the time goes:
time: 77.6 us; the launch traced here: 76.1 us
  Pallas kernels  38.4 us (49%)
  starting transfers between devices  19.1 us (25%)
  waiting for transfers between devices  9.13 us (12%)
  local copies, waits for them, and re-layouts  4.73 us (6%)
  other arithmetic  4.58 us (6%)
    pallas_call x1, Pallas kernels, on_device(): pl.pallas_call(rest_kernel, grid=(3,), out_shape=[jax.ShapeDtypeStruct((r...  22.7 us
    ppermute x13, starting transfers between devices, shift_to(): lax.ppermute(value, axis, [(i, (i + by) % length) for i in range(length)])  19.1 us
    ppermute x13, waiting for transfers between devices, shift_to(): lax.ppermute(value, axis, [(i, (i + by) % length) for i in range(length)])  9.13 us
    pallas_call x1, Pallas kernels, on_device(): pl.pallas_call(own_kernel, out_shape=jax.ShapeDtypeStruct((piece, L), F32...  8.58 us
    pallas_call x1, Pallas kernels, on_device(): pl.pallas_call(window_kernel, out_shape=jax.ShapeDtypeStruct((stations, W...  3.95 us
    unnamed x22, local copies, waits for them, and re-layouts  3.9 us
    pallas_call x1, Pallas kernels, on_device(): pl.pallas_call(prep_kernel, out_shape=[jax.ShapeDtypeStruct((piece, 2 * L...  3.23 us
    div x1, other arithmetic, on_device(): return total / math.sqrt(stations * 16)  1.59 us
  transfers between devices with their start and end apart: 13, of which 5 were waited for; matrix products, arithmetic and copies ran while one was open for 6% of the time, Pallas kernels for 21%

commit v1 on v0

v1 whole, which is shorter than its diff:
```python
import functools
import math

import jax
import jax.numpy as jnp
from jax import lax
from jax.experimental import pallas as pl
from jax.experimental.pallas import tpu as pltpu
from jax.sharding import Mesh, PartitionSpec as P

TAPS = 64
D = 128
L = 256
WLEN = 384
BANDS = 4
LANE = 128
BF16 = jnp.bfloat16
F32 = jnp.float32
VMEM_LIMIT = 16 << 20


def vmem():
    return pl.BlockSpec(memory_space=pltpu.VMEM)


def smem():
    return pl.BlockSpec(memory_space=pltpu.SMEM)


def shift_to(value, axis, by):
    length = lax.axis_size(axis)
    return lax.ppermute(value, axis, [(i, (i + by) % length) for i in range(length)])


def near_peer(z):
    return z ^ 1


def far_peer(z):
    return 3 - z


def swap(value, peer):
    return lax.ppermute(value, "z", [(i, peer(i)) for i in range(4)])


def as_columns(rows, out):
    columns = jnp.transpose(rows.astype(F32))
    tail = columns[:, LANE:]
    out[:, 0:LANE] = columns[:, 0:LANE].astype(BF16)
    out[:, LANE : 2 * LANE] = jnp.concatenate([tail, tail - 1.0], axis=1).astype(BF16)


def as_lanes(row):
    return jnp.transpose(jnp.broadcast_to(row.astype(F32), (LANE, row.shape[1]))).astype(jnp.int32)


def delay_kernel(delays, own_send, own_keep, peer_both):
    z = lax.axis_index("z")
    width = delays.shape[1] // 4

    def rows_of(chunk):
        return delays[:, pl.ds(pl.multiple_of(chunk * width, LANE), width)]

    peer = near_peer(z)
    for i, chunk in enumerate((far_peer(peer), peer)):
        peer_both[:, i * width : (i + 1) * width] = rows_of(chunk).astype(F32).astype(BF16)
    as_columns(rows_of(far_peer(z)), own_send)
    as_columns(rows_of(z), own_keep)


def band_kernel(taps, starts, visibility, toeplitz, meta, circle):
    circle[...] = jnp.zeros_like(circle)
    circle[0:BANDS, 0:TAPS] = taps[...]
    turned = pltpu.roll(circle[...], 2 * LANE - TAPS + 1, axis=1)
    for b in range(BANDS):
        row = jnp.broadcast_to(turned[b : b + 1, :], (2 * LANE, 2 * LANE))
        band = pltpu.roll(row, 0, axis=1, stride=1, stride_axis=0)[:, 0:LANE]
        for part in range(3):
            rounded = band.astype(BF16)
            toeplitz[part, :, b * LANE : (b + 1) * LANE] = rounded
            band = band - rounded.astype(F32)
    tile = 2 * lax.axis_index("x") + lax.axis_index("core")
    meta[0] = as_lanes(starts[pl.ds(tile, 1), :]) + (LANE - TAPS + 1)
    meta[1] = as_lanes(visibility[pl.ds(tile, 1), :])


def window_kernel(gain, *refs):
    chips = 4
    mine, other = refs[:chips], refs[chips : 2 * chips]
    meta, toeplitz, out, line = refs[2 * chips :]
    x, core = lax.axis_index("x"), lax.axis_index("core")
    stations, samp = mine[0].shape
    tiles_in = (2 * chips * samp) // LANE
    line[:, 0:LANE] = jnp.zeros((stations, LANE), F32)
    line[:, (tiles_in + 1) * LANE :] = jnp.zeros((stations, LANE), F32)
    for k in range(chips):
        chip = lax.rem(x + chips - k, chips)
        for src, c in ((mine, core), (other, 1 - core)):
            at = pl.multiple_of((2 * chip + c) * samp + LANE, LANE)
            line[:, pl.ds(at, samp)] = src[k][...].astype(F32)
    first = meta[0]
    visible = meta[1].astype(F32)
    parts = [line[:, i * LANE : (i + 1) * LANE] for i in range(tiles_in + 2)]
    keep = WLEN // LANE + 2
    bit = 16
    while bit:
        size = min(len(parts), bit - 1 + keep)
        chosen = (first & (bit * LANE)) != 0
        parts = [
            jnp.where(chosen, parts[i + bit], parts[i]) if i + bit < len(parts) else parts[i]
            for i in range(size)
        ]
        bit //= 2
    span = jnp.concatenate(parts, axis=1)
    width = span.shape[1]
    bit = LANE // 2
    while bit:
        chosen = jnp.concatenate([(first & bit)] * (width // LANE), axis=1) != 0
        span = jnp.where(chosen, pltpu.roll(span, width - bit, axis=1), span)
        bit //= 2
    span = span.astype(BF16)
    blocks = jnp.concatenate([span[:, j * LANE : j * LANE + 2 * LANE] for j in range(WLEN // LANE)], axis=0)
    filtered = sum(jnp.dot(blocks, toeplitz[p], preferred_element_type=F32) for p in range(3))
    char = sum(gain[b] * jnp.square(filtered[:, b * LANE : (b + 1) * LANE]) for b in range(BANDS))
    char = char.astype(BF16).astype(F32)
    pieces = [char[j * stations : (j + 1) * stations] for j in range(WLEN // LANE)]
    mean = jnp.sum(sum(pieces), axis=1, keepdims=True) / WLEN
    for j, piece in enumerate(pieces):
        out[:, j * LANE : (j + 1) * LANE] = ((piece - mean) * visible).astype(BF16)


def one_hot(column, level):
    return jnp.where(column == jnp.asarray(level, BF16), jnp.asarray(1, BF16), jnp.asarray(0, BF16))


def fill_table(windows, table):
    w = windows[...]
    half = LANE // 2
    for d in range(D):
        rolled = pltpu.roll(w, (WLEN - d) % WLEN, axis=1)[:, 0:L]
        table[d * LANE : (d + 1) * LANE, :] = rolled[0:LANE]
        table[D * LANE + d * half : D * LANE + (d + 1) * half, :] = rolled[LANE:]


def pick_rows(columns, table):
    head, tail = columns[:, 0:LANE], columns[:, LANE : 2 * LANE]
    picks = [one_hot(head, d) for d in range(D)] + [one_hot(tail, d) for d in range(0, D, 2)]
    return jnp.dot(jnp.concatenate(picks, axis=1), table[...], preferred_element_type=F32)


def own_send_kernel(columns, windows, out, table):
    fill_table(windows, table)
    out[...] = pick_rows(columns, table)


def peer_send_kernel(delay_rows, windows, acc, out, table, keep_columns, columns):
    half = delay_rows.shape[1] // 2
    as_columns(delay_rows[:, 0:half], columns)
    as_columns(delay_rows[:, half:], keep_columns)
    fill_table(windows, table)
    out[...] = (acc[...] + pick_rows(columns, table)).astype(BF16)


def own_keep_kernel(columns, table, out):
    out[...] = pick_rows(columns, table)


def block_at(y, rows):
    return pl.ds(pl.multiple_of(lax.rem(y, 4) * rows, rows), rows)


def peer_keep_kernel(scale, columns, table, acc, received, *sends):
    y = lax.axis_index("y")
    rows = sends[0].shape[0]
    blocks = [block_at(y + k + 1, rows) for k in range(len(sends))]
    picked = pick_rows(jnp.concatenate([columns[b, :] for b in blocks], axis=0), table)
    for k, (b, send) in enumerate(zip(blocks, sends)):
        done = acc[b, :] + received[b, :].astype(F32)
        send[...] = ((done + picked[k * rows : (k + 1) * rows]) * scale).astype(BF16)


def last_kernel(scale, columns, table, acc, received, out):
    rows = out.shape[0]
    b = block_at(lax.axis_index("y"), rows)
    done = acc[b, :] + received[b, :].astype(F32)
    out[...] = (done + pick_rows(columns[b, :], table)) * scale


def cost(flops, size):
    return pl.CostEstimate(flops=flops, bytes_accessed=size, transcendentals=0)


def on_device(traces, fir_taps, band_gain, starts, delays, visibility):
    stations, samp = traces.shape
    piece = delays.shape[1] // 4
    shape = jax.ShapeDtypeStruct
    params = pltpu.CompilerParams(vmem_limit_bytes=VMEM_LIMIT)

    near = [traces] + [shift_to(traces, "x", k) for k in (1, 2, 3)]
    own_send, own_keep, peer_both = pl.pallas_call(
        delay_kernel,
        out_shape=[
            shape((piece, 2 * LANE), BF16),
            shape((piece, 2 * LANE), BF16),
            shape((stations, 2 * piece), BF16),
        ],
        in_specs=[vmem()],
        out_specs=[vmem()] * 3,
        compiler_params=params,
        cost_estimate=cost(1 << 32, 4 << 20),
        name="delay",
    )(delays)
    toeplitz, meta = pl.pallas_call(
        band_kernel,
        out_shape=[shape((3, 2 * LANE, BANDS * LANE), BF16), shape((2, stations, LANE), jnp.int32)],
        in_specs=[vmem()] * 3,
        out_specs=[vmem()] * 2,
        scratch_shapes=[pltpu.VMEM((8, 2 * LANE), F32)],
        compiler_params=params,
        cost_estimate=cost(1 << 31, 1 << 20),
        name="band",
    )(fir_taps, starts.T, visibility.T)
    peer_rows = swap(peer_both, near_peer)
    near, toeplitz, _ = lax.optimization_barrier((near, toeplitz, peer_both))
    other = [shift_to(block, "core", 1) for block in near]

    windows = pl.pallas_call(
        window_kernel,
        out_shape=shape((stations, WLEN), BF16),
        in_specs=[smem()] + [vmem()] * 10,
        out_specs=vmem(),
        scratch_shapes=[pltpu.VMEM((stations, 8 * samp + 2 * LANE), F32)],
        compiler_params=params,
        cost_estimate=cost(1 << 20, 1 << 16),
        name="window",
    )(band_gain, *near, *other, meta, toeplitz)
    peer_windows = swap(windows, near_peer)

    rows = piece // 4
    scale = 1.0 / math.sqrt(stations * 16)
    table = shape((stations * D, L), BF16)
    flat = shape((piece, 2 * LANE), BF16)
    whole, block, rounded = shape((piece, L), F32), shape((rows, L), F32), shape((rows, L), BF16)

    def stack(kernel, name, count, outs, args, scratch=()):
        return pl.pallas_call(
            kernel,
            out_shape=outs,
            in_specs=[vmem()] * len(args),
            out_specs=[vmem()] * len(outs),
            scratch_shapes=list(scratch),
            compiler_params=params,
            cost_estimate=cost(1 << 20, 1 << 16),
            name=name,
        )(*args)

    acc, own_table = stack(own_send_kernel, "own_send", piece, [whole, table], [own_send, windows])
    away, peer_table, peer_keep = stack(
        peer_send_kernel,
        "peer_send",
        piece,
        [shape((piece, L), BF16), table, flat],
        [peer_rows, peer_windows, acc],
        [pltpu.VMEM(flat.shape, flat.dtype)],
    )
    arrived = swap(away, far_peer)
    (acc,) = stack(own_keep_kernel, "own_keep", piece, [whole], [own_keep, own_table])
    args = [peer_keep, peer_table, acc, arrived]
    sends = stack(functools.partial(peer_keep_kernel, scale), "peer_keep", 3 * rows, [rounded] * 3, args)
    (kept,) = stack(functools.partial(last_kernel, scale), "last", rows, [block], args)
    received = [shift_to(send, "y", k + 1) for k, send in enumerate(sends)]
    return kept + sum(r.astype(F32) for r in received)


def solution(mesh):
    split = Mesh(mesh.devices.reshape(4, 4, 4, 2), ("z", "y", "x", "core"))
    sta, tile = ("z", "y"), ("x", "core")
    placed = (P(sta, tile), P(), P(), P(sta, None), P(sta, tile), P(sta, None))
    return jax.shard_map(
        on_device, mesh=split, in_specs=placed, out_specs=P(("x", "core", "z", "y"), None), check_vma=False
    )
```

time: 77.6 us -> 55.3 us (0.71); the launches traced: 76.1 us -> 55.2 us
  Pallas kernels: 38.4 us -> 30.1 us
  other arithmetic: 4.58 us -> 0.68 us
  waiting for transfers between devices: 9.13 us -> 5.44 us
  local copies, waits for them, and re-layouts: 4.73 us -> 1.43 us
  starting transfers between devices: 19.1 us -> 17.4 us
    ppermute x13 -> x10, starting transfers between devices: 19.1 us -> 10.4 us  [shift_to(): lax.ppermute(value, axis, [(i, (i + by) % length) for i in range(length)])]
    pallas_call x4 -> x8, Pallas kernels: 38.4 us -> 30.1 us  [the longest x5 27.2 us: stack(): pl.pallas_call(kernel, out_shape=outs, in_specs=[vmem()] * len(args), out...]
    ppermute x0 -> x3, starting transfers between devices: none -> 7 us  [swap(): return lax.ppermute(value, 'z', [(i, peer(i)) for i in range(4)])]
    ppermute x13 -> x10, waiting for transfers between devices: 9.13 us -> 5.19 us  [shift_to(): lax.ppermute(value, axis, [(i, (i + by) % length) for i in range(length)])]
    unnamed x22 -> x12, local copies, waits for them, and re-layouts: 3.9 us -> 1.43 us
    another operation x2 -> x0, other arithmetic: 1.64 us -> none  [the longest x1 1 us: on_device(): mine = jnp.stack(near)]
    div x1 -> x0, other arithmetic: 1.59 us -> none  [on_device(): return total / math.sqrt(stations * 16)]
    concatenate x1 -> x0, other arithmetic: 1.35 us -> none  [on_device(): jnp.concatenate([fir_taps[:, TAPS - 1:], jnp.zeros((BANDS, 2 * LANE - TAP...]
  transfers between devices with their start and end apart: 13 -> 13, of which waited for: 5 -> 8; matrix products, arithmetic and copies ran while one was open for 6% -> 0% of each run, Pallas kernels for 21% -> 33%
where the time goes in v1:
time: 55.3 us; the launch traced here: 55.2 us
  Pallas kernels  30.1 us (54%)
  starting transfers between devices  17.4 us (31%)
  waiting for transfers between devices  5.44 us (10%)
  local copies, waits for them, and re-layouts  1.43 us (3%)
  other arithmetic  0.68 us (1%)
    pallas_call x5, Pallas kernels, stack(): pl.pallas_call(kernel, out_shape=outs, in_specs=[vmem()] * len(args), out...  27.2 us
    ppermute x10, starting transfers between devices, shift_to(): lax.ppermute(value, axis, [(i, (i + by) % length) for i in range(length)])  10.4 us
    ppermute x3, starting transfers between devices, swap(): return lax.ppermute(value, 'z', [(i, peer(i)) for i in range(4)])  7 us
    ppermute x10, waiting for transfers between devices, shift_to(): lax.ppermute(value, axis, [(i, (i + by) % length) for i in range(length)])  5.19 us
    pallas_call x1, Pallas kernels, on_device(): pl.pallas_call(window_kernel, out_shape=shape((stations, WLEN), BF16), in...  2.2 us
    unnamed x12, local copies, waits for them, and re-layouts  1.43 us
  transfers between devices with their start and end apart: 13, of which 8 were waited for; matrix products, arithmetic and copies ran while one was open for 0% of the time, Pallas kernels for 33%

profile of v1, /device:TPU:6, one launch (start us, length us, event | category | flops | bytes accessed | tf_op | source)
XLA Modules:
  0.0 55.2 jit_solution(8877390168605204608)
XLA Ops:
  0.0 0.0 copy-start
  0.0 0.0 copy-start.1
  0.0 1.4 %collective-permute-start.2 = (bf16[192,384]{1,0:T(8,128)(2,1)}, bf16[192,384]{1,0:T(8,128)(2,1)S(1)}, u32[]{:S(2)}, u32[]{:S(2)}) collective-permute-start(bf16[192,384]{1,0:T(8,128)(2,1)} %refs_0_), channel_id=1, source_target_pairs={{0,4},{2,6},{4,0},{6,2},{1,5},{3,7},{5,1},{7,3},{8,12},{10,14},{12... | collective-permute-start | bytes 442376 | tf_op jit(solution)/shard_map/ppermute | solution.py:32
  1.4 2.1 %collective-permute-start.1 = (bf16[192,384]{1,0:T(8,128)(2,1)}, bf16[192,384]{1,0:T(8,128)(2,1)S(1)}, u32[]{:S(2)}, u32[]{:S(2)}) collective-permute-start(bf16[192,384]{1,0:T(8,128)(2,1)} %refs_0_), channel_id=1, source_target_pairs={{0,2},{2,4},{4,6},{6,0},{1,3},{3,5},{5,7},{7,1},{8,10},{10,12},{12... | collective-permute-start | bytes 442376 | tf_op jit(solution)/shard_map/ppermute | solution.py:32
  3.5 0.0 collective-permute-start.3
  3.5 0.0 copy-start.2
  3.5 1.4 %copy-done.2 = s32[192,2048]{1,0:T(8,128)S(1)} copy-done((s32[192,2048]{1,0:T(8,128)S(1)}, s32[192,2048]{1,0:T(8,128)}, u32[]{:S(2)}) %copy-start.2) | copy-done | bytes 1572888
  4.9 0.0 copy-start.3
  4.9 0.0 copy-start.4
  4.9 0.0 copy-start.5
  4.9 0.4 delay.1
  5.3 2.0 %collective-permute-start = (bf16[192,1024]{1,0:T(8,128)(2,1)S(1)}, bf16[192,1024]{1,0:T(8,128)(2,1)S(1)}, u32[]{:S(2)}, u32[]{:S(2)}) collective-permute-start(bf16[192,1024]{1,0:T(8,128)(2,1)S(1)} %get-tuple-element.23), channel_id=1, source_target_pairs={{0,32},{32,0},{64,96},{96,64},{1,33},{33,1},{65,97},{97,65},{2,34}... | collective-permute-start | bytes 1179656 | tf_op jit(solution)/shard_map/ppermute | solution.py:44
  7.3 0.0 copy-done.3
  7.3 0.0 copy-done.4
  7.3 0.0 copy-done.5
  7.3 0.4 band.1
  7.7 0.7 %collective-permute-done.2.refs_2_ = bf16[192,384]{1,0:T(8,128)(2,1)S(1)} collective-permute-done((bf16[192,384]{1,0:T(8,128)(2,1)}, bf16[192,384]{1,0:T(8,128)(2,1)S(1)}, u32[]{:S(2)}, u32[]{:S(2)}) %collective-permute-start.2) | collective-permute-done | bytes 147488 | tf_op jit(solution)/shard_map/ppermute | solution.py:32
  8.5 0.0 collective-permute-done.1.refs_1_
  8.5 2.3 %collective-permute-done.3.refs_3_ = bf16[192,384]{1,0:T(8,128)(2,1)S(1)} collective-permute-done((bf16[192,384]{1,0:T(8,128)(2,1)}, bf16[192,384]{1,0:T(8,128)(2,1)S(1)}, u32[]{:S(2)}, u32[]{:S(2)}) %collective-permute-start.3) | collective-permute-done | bytes 147488 | tf_op jit(solution)/shard_map/ppermute | solution.py:32
  10.8 0.0 copy-done
  10.8 0.0 collective-permute-start.4
  10.8 0.5 collective-permute-start.5
  11.3 0.0 collective-permute-start.6
  11.3 0.5 collective-permute-start.7
  11.8 0.3 collective-permute-done.4.refs_4_
  12.2 0.2 collective-permute-done.5.refs_5_
  12.4 0.3 collective-permute-done.6.refs_6_
  12.7 0.2 collective-permute-done.7.refs_7_
  12.9 0.0 copy-done.1
  12.9 2.2 %window.1.windows = bf16[192,384]{1,0:T(8,128)(2,1)S(1)} custom-call(f32[4]{0:T(128)S(1)} %copy-done.1, bf16[192,384]{1,0:T(8,128)(2,1)S(1)} %copy-done, bf16[192,384]{1,0:T(8,128)(2,1)S(1)} %collective-permute-done.1.refs_1_, bf16[192,384]{1,0:T(8,128)(2,1)S(1)} %collective-permute-done.2.refs_2_, bf16[192,384]{1,0:T(8,128)(2,1)S(1)} %collective-permute-done.3.refs_3_, ...), custom_call_target="tpu_custom_call" | custom-call | flops 1048576 | bytes 65536 | tf_op jit(solution)/shard_map/window/pallas_call | solution.py:228
  15.1 2.2 %collective-permute-start.8 = (bf16[192,384]{1,0:T(8,128)(2,1)S(1)}, bf16[192,384]{1,0:T(8,128)(2,1)S(1)}, u32[]{:S(2)}, u32[]{:S(2)}) collective-permute-start(bf16[192,384]{1,0:T(8,128)(2,1)S(1)} %window.1.windows), channel_id=1, source_target_pairs={{0,32},{32,0},{64,96},{96,64},{1,33},{33,1},{65,97},{97,65},{2,34}... | collective-permute-start | bytes 442376 | tf_op jit(solution)/shard_map/ppermute | solution.py:44
  17.3 6.8 %own_send.1 = (f32[512,256]{1,0:T(8,128)S(1)}, bf16[24576,256]{1,0:T(8,128)(2,1)S(1)}) custom-call(bf16[512,256]{1,0:T(8,128)(2,1)S(1)} %get-tuple-element.31.columns, bf16[192,384]{1,0:T(8,128)(2,1)S(1)} %window.1.windows), custom_call_target="tpu_custom_call" | custom-call | flops 1048576 | bytes 65536 | tf_op jit(solution)/shard_map/own_send/pallas_call | solution.py:247
  24.1 0.0 collective-permute-done.delay_rows
  24.1 0.0 collective-permute-done.8.windows
  24.1 6.9 %peer_send.1 = (bf16[512,256]{1,0:T(8,128)(2,1)S(1)}, bf16[24576,256]{1,0:T(8,128)(2,1)S(1)}, bf16[512,256]{1,0:T(8,128)(2,1)S(1)}) custom-call(bf16[192,1024]{1,0:T(8,128)(2,1)S(1)} %collective-permute-done.delay_rows, bf16[192,384]{1,0:T(8,128)(2,1)S(1)} %collective-permute-done.8.windows, f32[512,256]{1,0:T(8,128)S(1)} %get-tuple-element.32.acc), custom_call_target="tpu_custom_call" | custom-call | flops 1048576 | bytes 65536 | tf_op jit(solution)/shard_map/peer_send/pallas_call | solution.py:247
  30.9 2.8 %collective-permute-start.9 = (bf16[512,256]{1,0:T(8,128)(2,1)S(1)}, bf16[512,256]{1,0:T(8,128)(2,1)S(1)}, u32[]{:S(2)}, u32[]{:S(2)}) collective-permute-start(bf16[512,256]{1,0:T(8,128)(2,1)S(1)} %get-tuple-element.37), channel_id=1, source_target_pairs={{0,96},{32,64},{64,32},{96,0},{1,97},{33,65},{65,33},{97,1},{2,98}... | collective-permute-start | bytes 786440 | tf_op jit(solution)/shard_map/ppermute | solution.py:44
  33.8 6.7 %own_keep.1.acc = f32[512,256]{1,0:T(8,128)S(1)} custom-call(bf16[512,256]{1,0:T(8,128)(2,1)S(1)} %get-tuple-element.35.columns, bf16[24576,256]{1,0:T(8,128)(2,1)S(1)} %get-tuple-element.36.table), custom_call_target="tpu_custom_call" | custom-call | flops 1048576 | bytes 65536 | tf_op jit(solution)/shard_map/own_keep/pallas_call | solution.py:247
  40.4 0.2 collective-permute-done.9.received
  40.7 5.0 %peer_keep.1 = (bf16[128,256]{1,0:T(8,128)(2,1)S(1)}, bf16[128,256]{1,0:T(8,128)(2,1)S(1)}, bf16[128,256]{1,0:T(8,128)(2,1)S(1)}) custom-call(bf16[512,256]{1,0:T(8,128)(2,1)S(1)} %get-tuple-element.33.columns, bf16[24576,256]{1,0:T(8,128)(2,1)S(1)} %get-tuple-element.34.table, f32[512,256]{1,0:T(8,128)S(1)} %own_keep.1.acc, ...), custom_call_target="tpu_custom_call" | custom-call | flops 1048576 | bytes 65536 | tf_op jit(solution)/shard_map/peer_keep/pallas_call | solution.py:247
  45.7 1.6 %collective-permute-start.10 = (bf16[128,256]{1,0:T(8,128)(2,1)S(1)}, bf16[128,256]{1,0:T(8,128)(2,1)S(1)}, u32[]{:S(2)}, u32[]{:S(2)}) collective-permute-start(bf16[128,256]{1,0:T(8,128)(2,1)S(1)} %get-tuple-element.38), channel_id=1, source_target_pairs={{0,8},{8,16},{16,24},{24,0},{1,9},{9,17},{17,25},{25,1},{2,10},{10... | collective-permute-start | bytes 196616 | tf_op jit(solution)/shard_map/ppermute | solution.py:32
  47.4 2.9 %collective-permute-start.11 = (bf16[128,256]{1,0:T(8,128)(2,1)S(1)}, bf16[128,256]{1,0:T(8,128)(2,1)S(1)}, u32[]{:S(2)}, u32[]{:S(2)}) collective-permute-start(bf16[128,256]{1,0:T(8,128)(2,1)S(1)} %get-tuple-element.39), channel_id=1, source_target_pairs={{0,16},{8,24},{16,0},{24,8},{1,17},{9,25},{17,1},{25,9},{2,18},{10... | collective-permute-start | bytes 196616 | tf_op jit(solution)/shard_map/ppermute | solution.py:32
  50.3 1.3 %collective-permute-start.12 = (bf16[128,256]{1,0:T(8,128)(2,1)S(1)}, bf16[128,256]{1,0:T(8,128)(2,1)S(1)}, u32[]{:S(2)}, u32[]{:S(2)}) collective-permute-start(bf16[128,256]{1,0:T(8,128)(2,1)S(1)} %get-tuple-element.40), channel_id=1, source_target_pairs={{0,24},{8,0},{16,8},{24,16},{1,25},{9,1},{17,9},{25,17},{2,26},{10... | collective-permute-start | bytes 196616 | tf_op jit(solution)/shard_map/ppermute | solution.py:32
  51.6 1.8 %last.1 = f32[128,256]{1,0:T(8,128)S(1)} custom-call(bf16[512,256]{1,0:T(8,128)(2,1)S(1)} %get-tuple-element.33.columns, bf16[24576,256]{1,0:T(8,128)(2,1)S(1)} %get-tuple-element.34.table, f32[512,256]{1,0:T(8,128)S(1)} %own_keep.1.acc, bf16[512,256]{1,0:T(8,128)(2,1)S(1)} %collective-permute-done.9.received), custom_call_target="tpu_custom_call" | custom-call | flops 1048576 | bytes 65536 | tf_op jit(solution)/shard_map/last/pallas_call | solution.py:247
  53.4 0.0 collective-permute-done.10
  53.5 0.0 collective-permute-done.11
  53.5 1.1 %collective-permute-done.12 = bf16[128,256]{1,0:T(8,128)(2,1)S(1)} collective-permute-done((bf16[128,256]{1,0:T(8,128)(2,1)S(1)}, bf16[128,256]{1,0:T(8,128)(2,1)S(1)}, u32[]{:S(2)}, u32[]{:S(2)}) %collective-permute-start.12) | collective-permute-done | bytes 65568 | tf_op jit(solution)/shard_map/ppermute | solution.py:32
  54.5 0.7 %add_add_fusion = f32[128,256]{1,0:T(8,128)} fusion(f32[128,256]{1,0:T(8,128)S(1)} %last.1, bf16[128,256]{1,0:T(8,128)(2,1)S(1)} %collective-permute-done.12, bf16[128,256]{1,0:T(8,128)(2,1)S(1)} %collective-permute-done.11, bf16[128,256]{1,0:T(8,128)(2,1)S(1)} %collective-permute-done.10), kind=kLoop, calls=%fused_computation | loop fusion | flops 196608 | bytes 458752 | tf_op jit(solution)/shard_map/add | solution.py:273
Async XLA Ops:
  0.0 10.8 %copy-start = (bf16[192,384]{1,0:T(8,128)(2,1)S(1)}, bf16[192,384]{1,0:T(8,128)(2,1)}, u32[]{:S(2)}) copy-start(bf16[192,384]{1,0:T(8,128)(2,1)} %refs_0_) | copy-start | bytes 442372
  0.0 12.9 %copy-start.1 = (f32[4]{0:T(128)S(1)}, f32[4]{0:T(128)}, u32[]{:S(2)}) copy-start(f32[4]{0:T(128)} %gain.1) | copy-start | bytes 52
  0.0 8.4 %collective-permute-start.2 = (bf16[192,384]{1,0:T(8,128)(2,1)}, bf16[192,384]{1,0:T(8,128)(2,1)S(1)}, u32[]{:S(2)}, u32[]{:S(2)}) collective-permute-start(bf16[192,384]{1,0:T(8,128)(2,1)} %refs_0_), channel_id=1, source_target_pairs={{0,4},{2,6},{4,0},{6,2},{1,5},{3,7},{5,1},{7,3},{8,12},{10,14},{12... | collective-permute-start | bytes 442376 | tf_op jit(solution)/shard_map/ppermute | solution.py:32
  1.4 7.0 %collective-permute-start.1 = (bf16[192,384]{1,0:T(8,128)(2,1)}, bf16[192,384]{1,0:T(8,128)(2,1)S(1)}, u32[]{:S(2)}, u32[]{:S(2)}) collective-permute-start(bf16[192,384]{1,0:T(8,128)(2,1)} %refs_0_), channel_id=1, source_target_pairs={{0,2},{2,4},{4,6},{6,0},{1,3},{3,5},{5,7},{7,1},{8,10},{10,12},{12... | collective-permute-start | bytes 442376 | tf_op jit(solution)/shard_map/ppermute | solution.py:32
  3.5 7.3 %collective-permute-start.3 = (bf16[192,384]{1,0:T(8,128)(2,1)}, bf16[192,384]{1,0:T(8,128)(2,1)S(1)}, u32[]{:S(2)}, u32[]{:S(2)}) collective-permute-start(bf16[192,384]{1,0:T(8,128)(2,1)} %refs_0_), channel_id=1, source_target_pairs={{0,6},{2,0},{4,2},{6,4},{1,7},{3,1},{5,3},{7,5},{8,14},{10,8},{12,... | collective-permute-start | bytes 442376 | tf_op jit(solution)/shard_map/ppermute | solution.py:32
  3.5 1.4 %copy-start.2 = (s32[192,2048]{1,0:T(8,128)S(1)}, s32[192,2048]{1,0:T(8,128)}, u32[]{:S(2)}) copy-start(s32[192,2048]{1,0:T(8,128)} %delays.1) | copy-start | bytes 4718596
  4.9 2.4 %copy-start.3 = (s32[192,8]{0,1:T(8,128)S(1)}, s32[192,8]{0,1:T(8,128)}, u32[]{:S(2)}) copy-start(s32[192,8]{0,1:T(8,128)} %param.9) | copy-start | bytes 18436
  4.9 2.4 %copy-start.4 = (s32[192,8]{0,1:T(8,128)S(1)}, s32[192,8]{0,1:T(8,128)}, u32[]{:S(2)}) copy-start(s32[192,8]{0,1:T(8,128)} %param.11) | copy-start | bytes 18436
  4.9 2.4 %copy-start.5 = (f32[4,64]{1,0:T(4,128)S(1)}, f32[4,64]{1,0:T(4,128)}, u32[]{:S(2)}) copy-start(f32[4,64]{1,0:T(4,128)} %taps.1) | copy-start | bytes 3076
  5.3 18.7 %collective-permute-start = (bf16[192,1024]{1,0:T(8,128)(2,1)S(1)}, bf16[192,1024]{1,0:T(8,128)(2,1)S(1)}, u32[]{:S(2)}, u32[]{:S(2)}) collective-permute-start(bf16[192,1024]{1,0:T(8,128)(2,1)S(1)} %get-tuple-element.23), channel_id=1, source_target_pairs={{0,32},{32,0},{64,96},{96,64},{1,33},{33,1},{65,97},{97,65},{2,34}... | collective-permute-start | bytes 1179656 | tf_op jit(solution)/shard_map/ppermute | solution.py:44
  10.8 1.4 %collective-permute-start.4 = (bf16[192,384]{1,0:T(8,128)(2,1)S(1)}, bf16[192,384]{1,0:T(8,128)(2,1)S(1)}, u32[]{:S(2)}, u32[]{:S(2)}) collective-permute-start(bf16[192,384]{1,0:T(8,128)(2,1)S(1)} %copy-done), channel_id=1, source_target_pairs={{0,1},{1,0},{2,3},{3,2},{4,5},{5,4},{6,7},{7,6},{8,9},{9,8},{10,11... | collective-permute-start | bytes 442376 | tf_op jit(solution)/shard_map/ppermute | solution.py:32
  10.8 1.6 %collective-permute-start.5 = (bf16[192,384]{1,0:T(8,128)(2,1)S(1)}, bf16[192,384]{1,0:T(8,128)(2,1)S(1)}, u32[]{:S(2)}, u32[]{:S(2)}) collective-permute-start(bf16[192,384]{1,0:T(8,128)(2,1)S(1)} %collective-permute-done.1.refs_1_), channel_id=1, source_target_pairs={{0,1},{1,0},{2,3},{3,2},{4,5},{5,4},{6,7},{7,6},{8,9},{9,8},{10,11... | collective-permute-start | bytes 442376 | tf_op jit(solution)/shard_map/ppermute | solution.py:32
  11.3 1.4 %collective-permute-start.6 = (bf16[192,384]{1,0:T(8,128)(2,1)S(1)}, bf16[192,384]{1,0:T(8,128)(2,1)S(1)}, u32[]{:S(2)}, u32[]{:S(2)}) collective-permute-start(bf16[192,384]{1,0:T(8,128)(2,1)S(1)} %collective-permute-done.2.refs_2_), channel_id=1, source_target_pairs={{0,1},{1,0},{2,3},{3,2},{4,5},{5,4},{6,7},{7,6},{8,9},{9,8},{10,11... | collective-permute-start | bytes 442376 | tf_op jit(solution)/shard_map/ppermute | solution.py:32
  11.3 1.6 %collective-permute-start.7 = (bf16[192,384]{1,0:T(8,128)(2,1)S(1)}, bf16[192,384]{1,0:T(8,128)(2,1)S(1)}, u32[]{:S(2)}, u32[]{:S(2)}) collective-permute-start(bf16[192,384]{1,0:T(8,128)(2,1)S(1)} %collective-permute-done.3.refs_3_), channel_id=1, source_target_pairs={{0,1},{1,0},{2,3},{3,2},{4,5},{5,4},{6,7},{7,6},{8,9},{9,8},{10,11... | collective-permute-start | bytes 442376 | tf_op jit(solution)/shard_map/ppermute | solution.py:32
  15.1 9.0 %collective-permute-start.8 = (bf16[192,384]{1,0:T(8,128)(2,1)S(1)}, bf16[192,384]{1,0:T(8,128)(2,1)S(1)}, u32[]{:S(2)}, u32[]{:S(2)}) collective-permute-start(bf16[192,384]{1,0:T(8,128)(2,1)S(1)} %window.1.windows), channel_id=1, source_target_pairs={{0,32},{32,0},{64,96},{96,64},{1,33},{33,1},{65,97},{97,65},{2,34}... | collective-permute-start | bytes 442376 | tf_op jit(solution)/shard_map/ppermute | solution.py:44
  30.9 9.7 %collective-permute-start.9 = (bf16[512,256]{1,0:T(8,128)(2,1)S(1)}, bf16[512,256]{1,0:T(8,128)(2,1)S(1)}, u32[]{:S(2)}, u32[]{:S(2)}) collective-permute-start(bf16[512,256]{1,0:T(8,128)(2,1)S(1)} %get-tuple-element.37), channel_id=1, source_target_pairs={{0,96},{32,64},{64,32},{96,0},{1,97},{33,65},{65,33},{97,1},{2,98}... | collective-permute-start | bytes 786440 | tf_op jit(solution)/shard_map/ppermute | solution.py:44
  45.7 7.7 %collective-permute-start.10 = (bf16[128,256]{1,0:T(8,128)(2,1)S(1)}, bf16[128,256]{1,0:T(8,128)(2,1)S(1)}, u32[]{:S(2)}, u32[]{:S(2)}) collective-permute-start(bf16[128,256]{1,0:T(8,128)(2,1)S(1)} %get-tuple-element.38), channel_id=1, source_target_pairs={{0,8},{8,16},{16,24},{24,0},{1,9},{9,17},{17,25},{25,1},{2,10},{10... | collective-permute-start | bytes 196616 | tf_op jit(solution)/shard_map/ppermute | solution.py:32
  47.4 6.1 %collective-permute-start.11 = (bf16[128,256]{1,0:T(8,128)(2,1)S(1)}, bf16[128,256]{1,0:T(8,128)(2,1)S(1)}, u32[]{:S(2)}, u32[]{:S(2)}) collective-permute-start(bf16[128,256]{1,0:T(8,128)(2,1)S(1)} %get-tuple-element.39), channel_id=1, source_target_pairs={{0,16},{8,24},{16,0},{24,8},{1,17},{9,25},{17,1},{25,9},{2,18},{10... | collective-permute-start | bytes 196616 | tf_op jit(solution)/shard_map/ppermute | solution.py:32
  50.3 4.3 %collective-permute-start.12 = (bf16[128,256]{1,0:T(8,128)(2,1)S(1)}, bf16[128,256]{1,0:T(8,128)(2,1)S(1)}, u32[]{:S(2)}, u32[]{:S(2)}) collective-permute-start(bf16[128,256]{1,0:T(8,128)(2,1)S(1)} %get-tuple-element.40), channel_id=1, source_target_pairs={{0,24},{8,0},{16,8},{24,16},{1,25},{9,1},{17,9},{25,17},{2,26},{10... | collective-permute-start | bytes 196616 | tf_op jit(solution)/shard_map/ppermute | solution.py:32

commit v2 on v1

--- a/solution.py
+++ b/solution.py
@@ -9,14 +9,14 @@
 from jax.sharding import Mesh, PartitionSpec as P
 
 TAPS = 64
-D = 128
+HALF = 64
 L = 256
 WLEN = 384
 BANDS = 4
 LANE = 128
 BF16 = jnp.bfloat16
 F32 = jnp.float32
-VMEM_LIMIT = 16 << 20
+VMEM_LIMIT = 24 << 20
 
 
 def vmem():
@@ -44,13 +44,6 @@
     return lax.ppermute(value, "z", [(i, peer(i)) for i in range(4)])
 
 
-def as_columns(rows, out):
-    columns = jnp.transpose(rows.astype(F32))
-    tail = columns[:, LANE:]
-    out[:, 0:LANE] = columns[:, 0:LANE].astype(BF16)
-    out[:, LANE : 2 * LANE] = jnp.concatenate([tail, tail - 1.0], axis=1).astype(BF16)
-
-
 def as_lanes(row):
     return jnp.transpose(jnp.broadcast_to(row.astype(F32), (LANE, row.shape[1]))).astype(jnp.int32)
 
@@ -60,13 +53,13 @@
     width = delays.shape[1] // 4
 
     def rows_of(chunk):
-        return delays[:, pl.ds(pl.multiple_of(chunk * width, LANE), width)]
+        return delays[:, pl.ds(pl.multiple_of(chunk * width, LANE), width)].astype(F32).astype(BF16)
 
     peer = near_peer(z)
-    for i, chunk in enumerate((far_peer(peer), peer)):
-        peer_both[:, i * width : (i + 1) * width] = rows_of(chunk).astype(F32).astype(BF16)
-    as_columns(rows_of(far_peer(z)), own_send)
-    as_columns(rows_of(z), own_keep)
+    peer_both[:, 0:width] = rows_of(far_peer(peer))
+    peer_both[:, width : 2 * width] = rows_of(peer)
+    own_send[...] = rows_of(far_peer(z))
+    own_keep[...] = rows_of(z)
 
 
 def band_kernel(taps, starts, visibility, toeplitz, meta, circle):
@@ -130,61 +123,73 @@
         out[:, j * LANE : (j + 1) * LANE] = ((piece - mean) * visible).astype(BF16)
 
 
-def one_hot(column, level):
-    return jnp.where(column == jnp.asarray(level, BF16), jnp.asarray(1, BF16), jnp.asarray(0, BF16))
-
-
-def fill_table(windows, table):
-    w = windows[...]
-    half = LANE // 2
-    for d in range(D):
-        rolled = pltpu.roll(w, (WLEN - d) % WLEN, axis=1)[:, 0:L]
-        table[d * LANE : (d + 1) * LANE, :] = rolled[0:LANE]
-        table[D * LANE + d * half : D * LANE + (d + 1) * half, :] = rolled[LANE:]
-
-
-def pick_rows(columns, table):
-    head, tail = columns[:, 0:LANE], columns[:, LANE : 2 * LANE]
-    picks = [one_hot(head, d) for d in range(D)] + [one_hot(tail, d) for d in range(0, D, 2)]
-    return jnp.dot(jnp.concatenate(picks, axis=1), table[...], preferred_element_type=F32)
-
-
-def own_send_kernel(columns, windows, out, table):
-    fill_table(windows, table)
-    out[...] = pick_rows(columns, table)
-
-
-def peer_send_kernel(delay_rows, windows, acc, out, table, keep_columns, columns):
-    half = delay_rows.shape[1] // 2
-    as_columns(delay_rows[:, 0:half], columns)
-    as_columns(delay_rows[:, half:], keep_columns)
-    fill_table(windows, table)
-    out[...] = (acc[...] + pick_rows(columns, table)).astype(BF16)
-
-
-def own_keep_kernel(columns, table, out):
-    out[...] = pick_rows(columns, table)
-
-
-def block_at(y, rows):
-    return pl.ds(pl.multiple_of(lax.rem(y, 4) * rows, rows), rows)
-
-
-def peer_keep_kernel(scale, columns, table, acc, received, *sends):
-    y = lax.axis_index("y")
-    rows = sends[0].shape[0]
-    blocks = [block_at(y + k + 1, rows) for k in range(len(sends))]
-    picked = pick_rows(jnp.concatenate([columns[b, :] for b in blocks], axis=0), table)
-    for k, (b, send) in enumerate(zip(blocks, sends)):
-        done = acc[b, :] + received[b, :].astype(F32)
-        send[...] = ((done + picked[k * rows : (k + 1) * rows]) * scale).astype(BF16)
-
-
-def last_kernel(scale, columns, table, acc, received, out):
-    rows = out.shape[0]
-    b = block_at(lax.axis_index("y"), rows)
-    done = acc[b, :] + received[b, :].astype(F32)
-    out[...] = (done + pick_rows(columns[b, :], table)) * scale
+def one_hot(delay, level):
+    return jnp.where(delay == jnp.asarray(level, BF16), jnp.asarray(1, BF16), jnp.asarray(0, BF16))
+
+
+def fill_table(windows, table, plain, steps):
+    turned = jnp.transpose(windows[...].astype(F32))
+    rest = turned[:, LANE:]
+    plain[0] = turned[:, 0:LANE]
+    plain[1] = jnp.concatenate([rest, pltpu.roll(rest, WLEN - 1, axis=0)], axis=1)
+    for i in range(2):
+        steps[i] = plain[i, 0 : WLEN - HALF, :] - plain[i, HALF:WLEN, :]
+    for part, (source, first) in enumerate(((steps, 0), (plain, HALF), (steps, HALF))):
+        for tile in range(HALF + HALF // 2):
+            i, d = (0, tile) if tile < HALF else (1, 2 * (tile - HALF))
+            for k in range(2):
+                at = first + k * 2 * HALF + d
+                table[part, k * HALF : (k + 1) * HALF, tile * LANE : (tile + 1) * LANE] = source[
+                    i, at : at + HALF, :
+                ].astype(BF16)
+
+
+def pick_rows(delays, table):
+    shift = jnp.asarray(HALF, BF16)
+    low = jnp.where(delays >= shift, delays - shift, delays)
+
+    def product(part, values, base):
+        head, rest = values[0:LANE], values[LANE:]
+        rows = [one_hot(head, base + d) for d in range(HALF)] + [one_hot(rest, base + d) for d in range(HALF)]
+        return jnp.dot(table[part], jnp.concatenate(rows, axis=0), preferred_element_type=F32)
+
+    first, both, second = product(0, delays, 0), product(1, low, 0), product(2, delays, HALF)
+    blocks = []
+    for k in range(2):
+        here = slice(k * HALF, (k + 1) * HALF)
+        blocks += [both[here] + first[here], both[here] - second[here]]
+    return jnp.concatenate(blocks, axis=0)
+
+
+def own_send_kernel(delays, windows, out, table, plain, steps):
+    fill_table(windows, table, plain, steps)
+    out[...] = pick_rows(delays[...], table)
+
+
+def peer_send_kernel(delays, windows, acc, out, table, plain, steps):
+    fill_table(windows, table, plain, steps)
+    half = delays.shape[1] // 2
+    out[...] = (acc[...] + pick_rows(delays[:, 0:half], table)).astype(BF16)
+
+
+def own_keep_kernel(delays, table, out):
+    out[...] = pick_rows(delays[...], table)
+
+
+def peer_keep_kernel(scale, delays, table, acc, received, kept, *rest):
+    sends, total = rest[:-1], rest[-1]
+    half = delays.shape[1] // 2
+    rows = kept.shape[0]
+    done = acc[...] + received[...].astype(F32)
+    total[...] = (done + pick_rows(delays[:, half:], table)) * scale
+
+    def block(k):
+        at = lax.rem(lax.axis_index("y") + k, 4) * rows
+        return jnp.transpose(total[:, pl.ds(pl.multiple_of(at, rows), rows)])
+
+    for k, send in enumerate(sends):
+        send[...] = block(k + 1).astype(BF16)
+    kept[...] = block(0)
 
 
 def cost(flops, size):
@@ -201,8 +206,8 @@
     own_send, own_keep, peer_both = pl.pallas_call(
         delay_kernel,
         out_shape=[
-            shape((piece, 2 * LANE), BF16),
-            shape((piece, 2 * LANE), BF16),
+            shape((stations, piece), BF16),
+            shape((stations, piece), BF16),
             shape((stations, 2 * piece), BF16),
         ],
         in_specs=[vmem()],
@@ -239,11 +244,11 @@
 
     rows = piece // 4
     scale = 1.0 / math.sqrt(stations * 16)
-    table = shape((stations * D, L), BF16)
-    flat = shape((piece, 2 * LANE), BF16)
-    whole, block, rounded = shape((piece, L), F32), shape((rows, L), F32), shape((rows, L), BF16)
-
-    def stack(kernel, name, count, outs, args, scratch=()):
+    table = shape((3, LANE, stations * HALF), BF16)
+    whole, block, rounded = shape((L, piece), F32), shape((rows, L), F32), shape((rows, L), BF16)
+    turned = [pltpu.VMEM((2, WLEN, LANE), F32), pltpu.VMEM((2, WLEN - HALF, LANE), F32)]
+
+    def stack(kernel, name, outs, args, scratch=()):
         return pl.pallas_call(
             kernel,
             out_shape=outs,
@@ -255,20 +260,19 @@
             name=name,
         )(*args)
 
-    acc, own_table = stack(own_send_kernel, "own_send", piece, [whole, table], [own_send, windows])
-    away, peer_table, peer_keep = stack(
-        peer_send_kernel,
-        "peer_send",
-        piece,
-        [shape((piece, L), BF16), table, flat],
-        [peer_rows, peer_windows, acc],
-        [pltpu.VMEM(flat.shape, flat.dtype)],
+    acc, own_table = stack(own_send_kernel, "own_send", [whole, table], [own_send, windows], turned)
+    away, peer_table = stack(
+        peer_send_kernel, "peer_send", [shape((L, piece), BF16), table], [peer_rows, peer_windows, acc], turned
     )
     arrived = swap(away, far_peer)
-    (acc,) = stack(own_keep_kernel, "own_keep", piece, [whole], [own_keep, own_table])
-    args = [peer_keep, peer_table, acc, arrived]
-    sends = stack(functools.partial(peer_keep_kernel, scale), "peer_keep", 3 * rows, [rounded] * 3, args)
-    (kept,) = stack(functools.partial(last_kernel, scale), "last", rows, [block], args)
+    (acc,) = stack(own_keep_kernel, "own_keep", [whole], [own_keep, own_table])
+    kept, *sends = stack(
+        functools.partial(peer_keep_kernel, scale),
+        "peer_keep",
+        [block] + [rounded] * 3,
+        [peer_rows, peer_table, acc, arrived],
+        [pltpu.VMEM(whole.shape, F32)],
+    )
     received = [shift_to(send, "y", k + 1) for k, send in enumerate(sends)]
     return kept + sum(r.astype(F32) for r in received)
 

time: 55.3 us -> 53.7 us (0.971)
  Pallas kernels: 30.1 us -> 24.8 us
  waiting for transfers between devices: 5.44 us -> 9.21 us
    pallas_call x5 -> x4, Pallas kernels: 27.2 us -> 22.1 us  [stack(): pl.pallas_call(kernel, out_shape=outs, in_specs=[vmem()] * len(args), out...]
    ppermute x10, waiting for transfers between devices: 5.19 us -> 7.37 us  [shift_to(): lax.ppermute(value, axis, [(i, (i + by) % length) for i in range(length)])]
    ppermute x3, waiting for transfers between devices: 0.25 us -> 1.84 us  [swap(): return lax.ppermute(value, 'z', [(i, peer(i)) for i in range(4)])]
  transfers between devices with their start and end apart: 13 -> 13, of which waited for: 8 -> 10; matrix products, arithmetic and copies ran while one was open for 0% -> 0% of each run, Pallas kernels for 33% -> 25%
where the time goes in v2:
time: 53.7 us; the launch traced here: 53.6 us
  Pallas kernels  24.8 us (46%)
  starting transfers between devices  17.4 us (32%)
  waiting for transfers between devices  9.21 us (17%)
  local copies, waits for them, and re-layouts  1.43 us (3%)
  other arithmetic  0.69 us (1%)
    pallas_call x4, Pallas kernels, stack(): pl.pallas_call(kernel, out_shape=outs, in_specs=[vmem()] * len(args), out...  22.1 us
    ppermute x10, starting transfers between devices, shift_to(): lax.ppermute(value, axis, [(i, (i + by) % length) for i in range(length)])  10.4 us
    ppermute x10, waiting for transfers between devices, shift_to(): lax.ppermute(value, axis, [(i, (i + by) % length) for i in range(length)])  7.37 us
    ppermute x3, starting transfers between devices, swap(): return lax.ppermute(value, 'z', [(i, peer(i)) for i in range(4)])  7 us
    pallas_call x1, Pallas kernels, on_device(): pl.pallas_call(window_kernel, out_shape=shape((stations, WLEN), BF16), in...  2.2 us
    ppermute x3, waiting for transfers between devices, swap(): return lax.ppermute(value, 'z', [(i, peer(i)) for i in range(4)])  1.84 us
    unnamed x12, local copies, waits for them, and re-layouts  1.43 us
  transfers between devices with their start and end apart: 13, of which 10 were waited for; matrix products, arithmetic and copies ran while one was open for 0% of the time, Pallas kernels for 25%

profile of v2, /device:TPU:6, one launch (start us, length us, event | category | flops | bytes accessed | tf_op | source)
XLA Modules:
  0.0 53.6 jit_solution(5819285901242416793)
XLA Ops:
  0.0 0.0 copy-start
  0.0 0.0 copy-start.1
  0.0 1.4 %collective-permute-start.2 = (bf16[192,384]{1,0:T(8,128)(2,1)}, bf16[192,384]{1,0:T(8,128)(2,1)S(1)}, u32[]{:S(2)}, u32[]{:S(2)}) collective-permute-start(bf16[192,384]{1,0:T(8,128)(2,1)} %refs_0_), channel_id=1, source_target_pairs={{0,4},{2,6},{4,0},{6,2},{1,5},{3,7},{5,1},{7,3},{8,12},{10,14},{12... | collective-permute-start | bytes 442376 | tf_op jit(solution)/shard_map/ppermute | solution.py:32
  1.4 2.1 %collective-permute-start.1 = (bf16[192,384]{1,0:T(8,128)(2,1)}, bf16[192,384]{1,0:T(8,128)(2,1)S(1)}, u32[]{:S(2)}, u32[]{:S(2)}) collective-permute-start(bf16[192,384]{1,0:T(8,128)(2,1)} %refs_0_), channel_id=1, source_target_pairs={{0,2},{2,4},{4,6},{6,0},{1,3},{3,5},{5,7},{7,1},{8,10},{10,12},{12... | collective-permute-start | bytes 442376 | tf_op jit(solution)/shard_map/ppermute | solution.py:32
  3.5 0.0 collective-permute-start.3
  3.5 0.0 copy-start.2
  3.5 1.4 %copy-done.2 = s32[192,2048]{1,0:T(8,128)S(1)} copy-done((s32[192,2048]{1,0:T(8,128)S(1)}, s32[192,2048]{1,0:T(8,128)}, u32[]{:S(2)}) %copy-start.2) | copy-done | bytes 1572888
  4.9 0.0 copy-start.3
  4.9 0.0 copy-start.4
  4.9 0.0 copy-start.5
  4.9 0.1 delay.1
  5.0 2.0 %collective-permute-start = (bf16[192,1024]{1,0:T(8,128)(2,1)S(1)}, bf16[192,1024]{1,0:T(8,128)(2,1)S(1)}, u32[]{:S(2)}, u32[]{:S(2)}) collective-permute-start(bf16[192,1024]{1,0:T(8,128)(2,1)S(1)} %get-tuple-element.23), channel_id=1, source_target_pairs={{0,32},{32,0},{64,96},{96,64},{1,33},{33,1},{65,97},{97,65},{2,34}... | collective-permute-start | bytes 1179656 | tf_op jit(solution)/shard_map/ppermute | solution.py:44
  7.0 0.0 copy-done.3
  7.0 0.0 copy-done.4
  7.0 0.0 copy-done.5
  7.0 0.4 band.1
  7.4 1.1 %collective-permute-done.2.refs_2_ = bf16[192,384]{1,0:T(8,128)(2,1)S(1)} collective-permute-done((bf16[192,384]{1,0:T(8,128)(2,1)}, bf16[192,384]{1,0:T(8,128)(2,1)S(1)}, u32[]{:S(2)}, u32[]{:S(2)}) %collective-permute-start.2) | collective-permute-done | bytes 147488 | tf_op jit(solution)/shard_map/ppermute | solution.py:32
  8.5 0.0 collective-permute-done.1.refs_1_
  8.5 2.3 %collective-permute-done.3.refs_3_ = bf16[192,384]{1,0:T(8,128)(2,1)S(1)} collective-permute-done((bf16[192,384]{1,0:T(8,128)(2,1)}, bf16[192,384]{1,0:T(8,128)(2,1)S(1)}, u32[]{:S(2)}, u32[]{:S(2)}) %collective-permute-start.3) | collective-permute-done | bytes 147488 | tf_op jit(solution)/shard_map/ppermute | solution.py:32
  10.8 0.0 copy-done
  10.8 0.0 collective-permute-start.4
  10.8 0.5 collective-permute-start.5
  11.3 0.0 collective-permute-start.6
  11.3 0.5 collective-permute-start.7
  11.8 0.3 collective-permute-done.4.refs_4_
  12.2 0.2 collective-permute-done.5.refs_5_
  12.4 0.3 collective-permute-done.6.refs_6_
  12.7 0.2 collective-permute-done.7.refs_7_
  12.9 0.0 copy-done.1
  12.9 2.2 %window.1.windows = bf16[192,384]{1,0:T(8,128)(2,1)S(1)} custom-call(f32[4]{0:T(128)S(1)} %copy-done.1, bf16[192,384]{1,0:T(8,128)(2,1)S(1)} %copy-done, bf16[192,384]{1,0:T(8,128)(2,1)S(1)} %collective-permute-done.1.refs_1_, bf16[192,384]{1,0:T(8,128)(2,1)S(1)} %collective-permute-done.2.refs_2_, bf16[192,384]{1,0:T(8,128)(2,1)S(1)} %collective-permute-done.3.refs_3_, ...), custom_call_target="tpu_custom_call" | custom-call | flops 1048576 | bytes 65536 | tf_op jit(solution)/shard_map/window/pallas_call | solution.py:233
  15.1 2.2 %collective-permute-start.8 = (bf16[192,384]{1,0:T(8,128)(2,1)S(1)}, bf16[192,384]{1,0:T(8,128)(2,1)S(1)}, u32[]{:S(2)}, u32[]{:S(2)}) collective-permute-start(bf16[192,384]{1,0:T(8,128)(2,1)S(1)} %window.1.windows), channel_id=1, source_target_pairs={{0,32},{32,0},{64,96},{96,64},{1,33},{33,1},{65,97},{97,65},{2,34}... | collective-permute-start | bytes 442376 | tf_op jit(solution)/shard_map/ppermute | solution.py:44
  17.3 5.8 %own_send.1 = (f32[256,512]{1,0:T(8,128)S(1)}, bf16[3,128,12288]{2,1,0:T(8,128)(2,1)S(1)}) custom-call(bf16[192,512]{1,0:T(8,128)(2,1)S(1)} %get-tuple-element.31.delays, bf16[192,384]{1,0:T(8,128)(2,1)S(1)} %window.1.windows), custom_call_target="tpu_custom_call" | custom-call | flops 1048576 | bytes 65536 | tf_op jit(solution)/shard_map/own_send/pallas_call | solution.py:252
  23.1 0.0 collective-permute-done.delays
  23.1 0.0 collective-permute-done.8.windows
  23.1 5.9 %peer_send.1 = (bf16[256,512]{1,0:T(8,128)(2,1)S(1)}, bf16[3,128,12288]{2,1,0:T(8,128)(2,1)S(1)}) custom-call(bf16[192,1024]{1,0:T(8,128)(2,1)S(1)} %collective-permute-done.delays, bf16[192,384]{1,0:T(8,128)(2,1)S(1)} %collective-permute-done.8.windows, f32[256,512]{1,0:T(8,128)S(1)} %get-tuple-element.32.acc), custom_call_target="tpu_custom_call" | custom-call | flops 1048576 | bytes 65536 | tf_op jit(solution)/shard_map/peer_send/pallas_call | solution.py:252
  29.0 2.8 %collective-permute-start.9 = (bf16[256,512]{1,0:T(8,128)(2,1)S(1)}, bf16[256,512]{1,0:T(8,128)(2,1)S(1)}, u32[]{:S(2)}, u32[]{:S(2)}) collective-permute-start(bf16[256,512]{1,0:T(8,128)(2,1)S(1)} %get-tuple-element.36), channel_id=1, source_target_pairs={{0,96},{32,64},{64,32},{96,0},{1,97},{33,65},{65,33},{97,1},{2,98}... | collective-permute-start | bytes 786440 | tf_op jit(solution)/shard_map/ppermute | solution.py:44
  31.8 5.1 %own_keep.1.acc = f32[256,512]{1,0:T(8,128)S(1)} custom-call(bf16[192,512]{1,0:T(8,128)(2,1)S(1)} %get-tuple-element.34.delays, bf16[3,128,12288]{2,1,0:T(8,128)(2,1)S(1)} %get-tuple-element.35.table), custom_call_target="tpu_custom_call" | custom-call | flops 1048576 | bytes 65536 | tf_op jit(solution)/shard_map/own_keep/pallas_call | solution.py:252
  36.9 1.8 %collective-permute-done.9.received = bf16[256,512]{1,0:T(8,128)(2,1)S(1)} collective-permute-done((bf16[256,512]{1,0:T(8,128)(2,1)S(1)}, bf16[256,512]{1,0:T(8,128)(2,1)S(1)}, u32[]{:S(2)}, u32[]{:S(2)}) %collective-permute-start.9) | collective-permute-done | bytes 262176 | tf_op jit(solution)/shard_map/ppermute | solution.py:44
  38.8 5.3 %peer_keep.1 = (f32[128,256]{1,0:T(8,128)S(1)}, bf16[128,256]{1,0:T(8,128)(2,1)S(1)}, bf16[128,256]{1,0:T(8,128)(2,1)S(1)}, bf16[128,256]{1,0:T(8,128)(2,1)S(1)}) custom-call(bf16[192,1024]{1,0:T(8,128)(2,1)S(1)} %collective-permute-done.delays, bf16[3,128,12288]{2,1,0:T(8,128)(2,1)S(1)} %get-tuple-element.33.table, f32[256,512]{1,0:T(8,128)S(1)} %own_keep.1.acc, ...), custom_call_target="tpu_custom_call" | custom-call | flops 1048576 | bytes 65536 | tf_op jit(solution)/shard_map/peer_keep/pallas_call | solution.py:252
  44.1 1.6 %collective-permute-start.10 = (bf16[128,256]{1,0:T(8,128)(2,1)S(1)}, bf16[128,256]{1,0:T(8,128)(2,1)S(1)}, u32[]{:S(2)}, u32[]{:S(2)}) collective-permute-start(bf16[128,256]{1,0:T(8,128)(2,1)S(1)} %get-tuple-element.38), channel_id=1, source_target_pairs={{0,8},{8,16},{16,24},{24,0},{1,9},{9,17},{17,25},{25,1},{2,10},{10... | collective-permute-start | bytes 196616 | tf_op jit(solution)/shard_map/ppermute | solution.py:32
  45.7 2.9 %collective-permute-start.11 = (bf16[128,256]{1,0:T(8,128)(2,1)S(1)}, bf16[128,256]{1,0:T(8,128)(2,1)S(1)}, u32[]{:S(2)}, u32[]{:S(2)}) collective-permute-start(bf16[128,256]{1,0:T(8,128)(2,1)S(1)} %get-tuple-element.39), channel_id=1, source_target_pairs={{0,16},{8,24},{16,0},{24,8},{1,17},{9,25},{17,1},{25,9},{2,18},{10... | collective-permute-start | bytes 196616 | tf_op jit(solution)/shard_map/ppermute | solution.py:32
  48.6 1.3 %collective-permute-start.12 = (bf16[128,256]{1,0:T(8,128)(2,1)S(1)}, bf16[128,256]{1,0:T(8,128)(2,1)S(1)}, u32[]{:S(2)}, u32[]{:S(2)}) collective-permute-start(bf16[128,256]{1,0:T(8,128)(2,1)S(1)} %get-tuple-element.40), channel_id=1, source_target_pairs={{0,24},{8,0},{16,8},{24,16},{1,25},{9,1},{17,9},{25,17},{2,26},{10... | collective-permute-start | bytes 196616 | tf_op jit(solution)/shard_map/ppermute | solution.py:32
  50.0 0.4 collective-permute-done.10
  50.3 1.2 %collective-permute-done.11 = bf16[128,256]{1,0:T(8,128)(2,1)S(1)} collective-permute-done((bf16[128,256]{1,0:T(8,128)(2,1)S(1)}, bf16[128,256]{1,0:T(8,128)(2,1)S(1)}, u32[]{:S(2)}, u32[]{:S(2)}) %collective-permute-start.11) | collective-permute-done | bytes 65568 | tf_op jit(solution)/shard_map/ppermute | solution.py:32
  51.6 1.3 %collective-permute-done.12 = bf16[128,256]{1,0:T(8,128)(2,1)S(1)} collective-permute-done((bf16[128,256]{1,0:T(8,128)(2,1)S(1)}, bf16[128,256]{1,0:T(8,128)(2,1)S(1)}, u32[]{:S(2)}, u32[]{:S(2)}) %collective-permute-start.12) | collective-permute-done | bytes 65568 | tf_op jit(solution)/shard_map/ppermute | solution.py:32
  52.9 0.7 %add_add_fusion = f32[128,256]{1,0:T(8,128)} fusion(f32[128,256]{1,0:T(8,128)S(1)} %get-tuple-element.37, bf16[128,256]{1,0:T(8,128)(2,1)S(1)} %collective-permute-done.12, bf16[128,256]{1,0:T(8,128)(2,1)S(1)} %collective-permute-done.11, bf16[128,256]{1,0:T(8,128)(2,1)S(1)} %collective-permute-done.10), kind=kLoop, calls=%fused_computation | loop fusion | flops 196608 | bytes 458752 | tf_op jit(solution)/shard_map/add | solution.py:277
Async XLA Ops:
  0.0 10.8 %copy-start = (bf16[192,384]{1,0:T(8,128)(2,1)S(1)}, bf16[192,384]{1,0:T(8,128)(2,1)}, u32[]{:S(2)}) copy-start(bf16[192,384]{1,0:T(8,128)(2,1)} %refs_0_) | copy-start | bytes 442372
  0.0 12.9 %copy-start.1 = (f32[4]{0:T(128)S(1)}, f32[4]{0:T(128)}, u32[]{:S(2)}) copy-start(f32[4]{0:T(128)} %gain.1) | copy-start | bytes 52
  0.0 8.4 %collective-permute-start.2 = (bf16[192,384]{1,0:T(8,128)(2,1)}, bf16[192,384]{1,0:T(8,128)(2,1)S(1)}, u32[]{:S(2)}, u32[]{:S(2)}) collective-permute-start(bf16[192,384]{1,0:T(8,128)(2,1)} %refs_0_), channel_id=1, source_target_pairs={{0,4},{2,6},{4,0},{6,2},{1,5},{3,7},{5,1},{7,3},{8,12},{10,14},{12... | collective-permute-start | bytes 442376 | tf_op jit(solution)/shard_map/ppermute | solution.py:32
  1.4 7.0 %collective-permute-start.1 = (bf16[192,384]{1,0:T(8,128)(2,1)}, bf16[192,384]{1,0:T(8,128)(2,1)S(1)}, u32[]{:S(2)}, u32[]{:S(2)}) collective-permute-start(bf16[192,384]{1,0:T(8,128)(2,1)} %refs_0_), channel_id=1, source_target_pairs={{0,2},{2,4},{4,6},{6,0},{1,3},{3,5},{5,7},{7,1},{8,10},{10,12},{12... | collective-permute-start | bytes 442376 | tf_op jit(solution)/shard_map/ppermute | solution.py:32
  3.5 7.3 %collective-permute-start.3 = (bf16[192,384]{1,0:T(8,128)(2,1)}, bf16[192,384]{1,0:T(8,128)(2,1)S(1)}, u32[]{:S(2)}, u32[]{:S(2)}) collective-permute-start(bf16[192,384]{1,0:T(8,128)(2,1)} %refs_0_), channel_id=1, source_target_pairs={{0,6},{2,0},{4,2},{6,4},{1,7},{3,1},{5,3},{7,5},{8,14},{10,8},{12,... | collective-permute-start | bytes 442376 | tf_op jit(solution)/shard_map/ppermute | solution.py:32
  3.5 1.4 %copy-start.2 = (s32[192,2048]{1,0:T(8,128)S(1)}, s32[192,2048]{1,0:T(8,128)}, u32[]{:S(2)}) copy-start(s32[192,2048]{1,0:T(8,128)} %delays.1) | copy-start | bytes 4718596
  4.9 2.1 %copy-start.3 = (s32[192,8]{0,1:T(8,128)S(1)}, s32[192,8]{0,1:T(8,128)}, u32[]{:S(2)}) copy-start(s32[192,8]{0,1:T(8,128)} %param.9) | copy-start | bytes 18436
  4.9 2.1 %copy-start.4 = (s32[192,8]{0,1:T(8,128)S(1)}, s32[192,8]{0,1:T(8,128)}, u32[]{:S(2)}) copy-start(s32[192,8]{0,1:T(8,128)} %param.11) | copy-start | bytes 18436
  4.9 2.1 %copy-start.5 = (f32[4,64]{1,0:T(4,128)S(1)}, f32[4,64]{1,0:T(4,128)}, u32[]{:S(2)}) copy-start(f32[4,64]{1,0:T(4,128)} %taps.1) | copy-start | bytes 3076
  5.0 18.1 %collective-permute-start = (bf16[192,1024]{1,0:T(8,128)(2,1)S(1)}, bf16[192,1024]{1,0:T(8,128)(2,1)S(1)}, u32[]{:S(2)}, u32[]{:S(2)}) collective-permute-start(bf16[192,1024]{1,0:T(8,128)(2,1)S(1)} %get-tuple-element.23), channel_id=1, source_target_pairs={{0,32},{32,0},{64,96},{96,64},{1,33},{33,1},{65,97},{97,65},{2,34}... | collective-permute-start | bytes 1179656 | tf_op jit(solution)/shard_map/ppermute | solution.py:44
  10.8 1.4 %collective-permute-start.4 = (bf16[192,384]{1,0:T(8,128)(2,1)S(1)}, bf16[192,384]{1,0:T(8,128)(2,1)S(1)}, u32[]{:S(2)}, u32[]{:S(2)}) collective-permute-start(bf16[192,384]{1,0:T(8,128)(2,1)S(1)} %copy-done), channel_id=1, source_target_pairs={{0,1},{1,0},{2,3},{3,2},{4,5},{5,4},{6,7},{7,6},{8,9},{9,8},{10,11... | collective-permute-start | bytes 442376 | tf_op jit(solution)/shard_map/ppermute | solution.py:32
  10.8 1.6 %collective-permute-start.5 = (bf16[192,384]{1,0:T(8,128)(2,1)S(1)}, bf16[192,384]{1,0:T(8,128)(2,1)S(1)}, u32[]{:S(2)}, u32[]{:S(2)}) collective-permute-start(bf16[192,384]{1,0:T(8,128)(2,1)S(1)} %collective-permute-done.1.refs_1_), channel_id=1, source_target_pairs={{0,1},{1,0},{2,3},{3,2},{4,5},{5,4},{6,7},{7,6},{8,9},{9,8},{10,11... | collective-permute-start | bytes 442376 | tf_op jit(solution)/shard_map/ppermute | solution.py:32
  11.3 1.4 %collective-permute-start.6 = (bf16[192,384]{1,0:T(8,128)(2,1)S(1)}, bf16[192,384]{1,0:T(8,128)(2,1)S(1)}, u32[]{:S(2)}, u32[]{:S(2)}) collective-permute-start(bf16[192,384]{1,0:T(8,128)(2,1)S(1)} %collective-permute-done.2.refs_2_), channel_id=1, source_target_pairs={{0,1},{1,0},{2,3},{3,2},{4,5},{5,4},{6,7},{7,6},{8,9},{9,8},{10,11... | collective-permute-start | bytes 442376 | tf_op jit(solution)/shard_map/ppermute | solution.py:32
  11.3 1.6 %collective-permute-start.7 = (bf16[192,384]{1,0:T(8,128)(2,1)S(1)}, bf16[192,384]{1,0:T(8,128)(2,1)S(1)}, u32[]{:S(2)}, u32[]{:S(2)}) collective-permute-start(bf16[192,384]{1,0:T(8,128)(2,1)S(1)} %collective-permute-done.3.refs_3_), channel_id=1, source_target_pairs={{0,1},{1,0},{2,3},{3,2},{4,5},{5,4},{6,7},{7,6},{8,9},{9,8},{10,11... | collective-permute-start | bytes 442376 | tf_op jit(solution)/shard_map/ppermute | solution.py:32
  15.1 8.0 %collective-permute-start.8 = (bf16[192,384]{1,0:T(8,128)(2,1)S(1)}, bf16[192,384]{1,0:T(8,128)(2,1)S(1)}, u32[]{:S(2)}, u32[]{:S(2)}) collective-permute-start(bf16[192,384]{1,0:T(8,128)(2,1)S(1)} %window.1.windows), channel_id=1, source_target_pairs={{0,32},{32,0},{64,96},{96,64},{1,33},{33,1},{65,97},{97,65},{2,34}... | collective-permute-start | bytes 442376 | tf_op jit(solution)/shard_map/ppermute | solution.py:44
  29.0 9.7 %collective-permute-start.9 = (bf16[256,512]{1,0:T(8,128)(2,1)S(1)}, bf16[256,512]{1,0:T(8,128)(2,1)S(1)}, u32[]{:S(2)}, u32[]{:S(2)}) collective-permute-start(bf16[256,512]{1,0:T(8,128)(2,1)S(1)} %get-tuple-element.36), channel_id=1, source_target_pairs={{0,96},{32,64},{64,32},{96,0},{1,97},{33,65},{65,33},{97,1},{2,98}... | collective-permute-start | bytes 786440 | tf_op jit(solution)/shard_map/ppermute | solution.py:44
  44.1 6.2 %collective-permute-start.10 = (bf16[128,256]{1,0:T(8,128)(2,1)S(1)}, bf16[128,256]{1,0:T(8,128)(2,1)S(1)}, u32[]{:S(2)}, u32[]{:S(2)}) collective-permute-start(bf16[128,256]{1,0:T(8,128)(2,1)S(1)} %get-tuple-element.38), channel_id=1, source_target_pairs={{0,8},{8,16},{16,24},{24,0},{1,9},{9,17},{17,25},{25,1},{2,10},{10... | collective-permute-start | bytes 196616 | tf_op jit(solution)/shard_map/ppermute | solution.py:32
  45.7 5.8 %collective-permute-start.11 = (bf16[128,256]{1,0:T(8,128)(2,1)S(1)}, bf16[128,256]{1,0:T(8,128)(2,1)S(1)}, u32[]{:S(2)}, u32[]{:S(2)}) collective-permute-start(bf16[128,256]{1,0:T(8,128)(2,1)S(1)} %get-tuple-element.39), channel_id=1, source_target_pairs={{0,16},{8,24},{16,0},{24,8},{1,17},{9,25},{17,1},{25,9},{2,18},{10... | collective-permute-start | bytes 196616 | tf_op jit(solution)/shard_map/ppermute | solution.py:32
  48.6 4.3 %collective-permute-start.12 = (bf16[128,256]{1,0:T(8,128)(2,1)S(1)}, bf16[128,256]{1,0:T(8,128)(2,1)S(1)}, u32[]{:S(2)}, u32[]{:S(2)}) collective-permute-start(bf16[128,256]{1,0:T(8,128)(2,1)S(1)} %get-tuple-element.40), channel_id=1, source_target_pairs={{0,24},{8,0},{16,8},{24,16},{1,25},{9,1},{17,9},{25,17},{2,26},{10... | collective-permute-start | bytes 196616 | tf_op jit(solution)/shard_map/ppermute | solution.py:32

commit v3 on v2

--- a/solution.py
+++ b/solution.py
@@ -32,16 +32,16 @@
     return lax.ppermute(value, axis, [(i, (i + by) % length) for i in range(length)])
 
 
-def near_peer(z):
-    return z ^ 1
-
-
-def far_peer(z):
-    return 3 - z
-
-
-def swap(value, peer):
-    return lax.ppermute(value, "z", [(i, peer(i)) for i in range(4)])
+def near_peer(i):
+    return i ^ 1
+
+
+def far_peer(i):
+    return 3 - i
+
+
+def swap(value, axis, peer):
+    return lax.ppermute(value, axis, [(i, peer(i)) for i in range(4)])
 
 
 def as_lanes(row):
@@ -172,24 +172,46 @@
     out[...] = (acc[...] + pick_rows(delays[:, 0:half], table)).astype(BF16)
 
 
-def own_keep_kernel(delays, table, out):
-    out[...] = pick_rows(delays[...], table)
-
-
-def peer_keep_kernel(scale, delays, table, acc, received, kept, *rest):
-    sends, total = rest[:-1], rest[-1]
-    half = delays.shape[1] // 2
+def y_blocks(ref, *owners):
+    rows = ref.shape[1] // 4
+    return jnp.concatenate([ref[:, pl.ds(pl.multiple_of(i * rows, rows), rows)] for i in owners], axis=1)
+
+
+def far_blocks(ref):
+    far = far_peer(lax.axis_index("y"))
+    return y_blocks(ref, far, near_peer(far))
+
+
+def near_blocks(ref):
+    y = lax.axis_index("y")
+    return y_blocks(ref, y, near_peer(y))
+
+
+def kept_half(ref):
+    return ref.at[:, pl.ds(ref.shape[1] // 2, ref.shape[1] // 2)]
+
+
+def first_keep_kernel(own_delays, own_table, peer_delays, peer_table, far, near, total):
+    total[...] = pick_rows(own_delays[...], own_table)
+    far[...] = far_blocks(total) + pick_rows(far_blocks(kept_half(peer_delays)), peer_table)
+    near[...] = near_blocks(total)
+
+
+def far_kernel(scale, far, received, out):
+    done = (far[...] + far_blocks(received).astype(F32)) * scale
+    out[...] = jnp.transpose(done).astype(BF16)
+
+
+def last_keep_kernel(scale, peer_delays, peer_table, near, received, out):
+    done = near[...] + near_blocks(received).astype(F32)
+    done = (done + pick_rows(near_blocks(kept_half(peer_delays)), peer_table)) * scale
+    out[...] = jnp.transpose(done)
+
+
+def near_kernel(done, received, kept, send):
     rows = kept.shape[0]
-    done = acc[...] + received[...].astype(F32)
-    total[...] = (done + pick_rows(delays[:, half:], table)) * scale
-
-    def block(k):
-        at = lax.rem(lax.axis_index("y") + k, 4) * rows
-        return jnp.transpose(total[:, pl.ds(pl.multiple_of(at, rows), rows)])
-
-    for k, send in enumerate(sends):
-        send[...] = block(k + 1).astype(BF16)
-    kept[...] = block(0)
+    kept[...] = done[0:rows] + received[0:rows].astype(F32)
+    send[...] = (done[rows:] + received[rows:].astype(F32)).astype(BF16)
 
 
 def cost(flops, size):
@@ -226,7 +248,7 @@
         cost_estimate=cost(1 << 31, 1 << 20),
         name="band",
     )(fir_taps, starts.T, visibility.T)
-    peer_rows = swap(peer_both, near_peer)
+    peer_rows = swap(peer_both, "z", near_peer)
     near, toeplitz, _ = lax.optimization_barrier((near, toeplitz, peer_both))
     other = [shift_to(block, "core", 1) for block in near]
 
@@ -240,7 +262,7 @@
         cost_estimate=cost(1 << 20, 1 << 16),
         name="window",
     )(band_gain, *near, *other, meta, toeplitz)
-    peer_windows = swap(windows, near_peer)
+    peer_windows = swap(windows, "z", near_peer)
 
     rows = piece // 4
     scale = 1.0 / math.sqrt(stations * 16)
@@ -248,7 +270,7 @@
     whole, block, rounded = shape((L, piece), F32), shape((rows, L), F32), shape((rows, L), BF16)
     turned = [pltpu.VMEM((2, WLEN, LANE), F32), pltpu.VMEM((2, WLEN - HALF, LANE), F32)]
 
-    def stack(kernel, name, outs, args, scratch=()):
+    def stack(kernel, name, outs, args, scratch=(), flops=1 << 20):
         return pl.pallas_call(
             kernel,
             out_shape=outs,
@@ -256,7 +278,7 @@
             out_specs=[vmem()] * len(outs),
             scratch_shapes=list(scratch),
             compiler_params=params,
-            cost_estimate=cost(1 << 20, 1 << 16),
+            cost_estimate=cost(flops, 1 << 16),
             name=name,
         )(*args)
 
@@ -264,17 +286,27 @@
     away, peer_table = stack(
         peer_send_kernel, "peer_send", [shape((L, piece), BF16), table], [peer_rows, peer_windows, acc], turned
     )
-    arrived = swap(away, far_peer)
-    (acc,) = stack(own_keep_kernel, "own_keep", [whole], [own_keep, own_table])
-    kept, *sends = stack(
-        functools.partial(peer_keep_kernel, scale),
-        "peer_keep",
-        [block] + [rounded] * 3,
-        [peer_rows, peer_table, acc, arrived],
+    arrived = swap(away, "z", far_peer)
+    half = shape((L, 2 * rows), F32)
+    far, near_rows = stack(
+        first_keep_kernel,
+        "first_keep",
+        [half, half],
+        [own_keep, own_table, peer_rows, peer_table],
         [pltpu.VMEM(whole.shape, F32)],
     )
-    received = [shift_to(send, "y", k + 1) for k, send in enumerate(sends)]
-    return kept + sum(r.astype(F32) for r in received)
+    (far,) = stack(functools.partial(far_kernel, scale), "far", [shape((2 * rows, L), BF16)], [far, arrived])
+    got = swap(far, "y", far_peer)
+    near_rows, _ = lax.optimization_barrier((near_rows, far))
+    (done,) = stack(
+        functools.partial(last_keep_kernel, scale),
+        "last_keep",
+        [shape((2 * rows, L), F32)],
+        [peer_rows, peer_table, near_rows, arrived],
+        flops=1 << 32,
+    )
+    kept, send = stack(near_kernel, "near", [block, rounded], [done, got])
+    return kept + swap(send, "y", near_peer).astype(F32)
 
 
 def solution(mesh):

time: 53.7 us -> 51.3 us (0.955)
  starting transfers between devices: 17.4 us -> 15 us
    ppermute x10 -> x7, starting transfers between devices: 10.4 us -> 4.52 us  [shift_to(): lax.ppermute(value, axis, [(i, (i + by) % length) for i in range(length)])]
    ppermute x3 -> x5, starting transfers between devices: 7 us -> 10.5 us  [swap(): return lax.ppermute(value, axis, [(i, peer(i)) for i in range(4)])]
    ppermute x10 -> x7, waiting for transfers between devices: 7.37 us -> 4.45 us  [shift_to(): lax.ppermute(value, axis, [(i, (i + by) % length) for i in range(length)])]
    ppermute x3 -> x5, waiting for transfers between devices: 1.84 us -> 4.66 us  [swap(): return lax.ppermute(value, axis, [(i, peer(i)) for i in range(4)])]
    pallas_call x4 -> x6, Pallas kernels: 22.1 us -> 22.2 us  [stack(): pl.pallas_call(kernel, out_shape=outs, in_specs=[vmem()] * len(args), out...]
  transfers between devices with their start and end apart: 13 -> 12, of which waited for: 10 -> 8; matrix products, arithmetic and copies ran while one was open for 0% -> 0% of each run, Pallas kernels for 25% -> 37%
where the time goes in v3:
time: 51.3 us; the launch traced here: 51.1 us
  Pallas kernels  24.8 us (48%)
  starting transfers between devices  15 us (29%)
  waiting for transfers between devices  9.11 us (18%)
  local copies, waits for them, and re-layouts  1.43 us (3%)
  other arithmetic  0.67 us (1%)
    pallas_call x6, Pallas kernels, stack(): pl.pallas_call(kernel, out_shape=outs, in_specs=[vmem()] * len(args), out...  22.2 us
    ppermute x5, starting transfers between devices, swap(): return lax.ppermute(value, axis, [(i, peer(i)) for i in range(4)])  10.5 us
    ppermute x5, waiting for transfers between devices, swap(): return lax.ppermute(value, axis, [(i, peer(i)) for i in range(4)])  4.66 us
    ppermute x7, starting transfers between devices, shift_to(): lax.ppermute(value, axis, [(i, (i + by) % length) for i in range(length)])  4.52 us
    ppermute x7, waiting for transfers between devices, shift_to(): lax.ppermute(value, axis, [(i, (i + by) % length) for i in range(length)])  4.45 us
    pallas_call x1, Pallas kernels, on_device(): pl.pallas_call(window_kernel, out_shape=shape((stations, WLEN), BF16), in...  2.2 us
    unnamed x12, local copies, waits for them, and re-layouts  1.43 us
  transfers between devices with their start and end apart: 12, of which 8 were waited for; matrix products, arithmetic and copies ran while one was open for 0% of the time, Pallas kernels for 37%

profile of v3, /device:TPU:6, one launch (start us, length us, event | category | flops | bytes accessed | tf_op | source)
XLA Modules:
  0.0 51.1 jit_solution(17788894822719702241)
XLA Ops:
  0.0 0.0 copy-start
  0.0 0.0 copy-start.1
  0.0 1.4 %collective-permute-start.2 = (bf16[192,384]{1,0:T(8,128)(2,1)}, bf16[192,384]{1,0:T(8,128)(2,1)S(1)}, u32[]{:S(2)}, u32[]{:S(2)}) collective-permute-start(bf16[192,384]{1,0:T(8,128)(2,1)} %refs_0_), channel_id=1, source_target_pairs={{0,4},{2,6},{4,0},{6,2},{1,5},{3,7},{5,1},{7,3},{8,12},{10,14},{12... | collective-permute-start | bytes 442376 | tf_op jit(solution)/shard_map/ppermute | solution.py:32
  1.4 2.1 %collective-permute-start.1 = (bf16[192,384]{1,0:T(8,128)(2,1)}, bf16[192,384]{1,0:T(8,128)(2,1)S(1)}, u32[]{:S(2)}, u32[]{:S(2)}) collective-permute-start(bf16[192,384]{1,0:T(8,128)(2,1)} %refs_0_), channel_id=1, source_target_pairs={{0,2},{2,4},{4,6},{6,0},{1,3},{3,5},{5,7},{7,1},{8,10},{10,12},{12... | collective-permute-start | bytes 442376 | tf_op jit(solution)/shard_map/ppermute | solution.py:32
  3.5 0.0 collective-permute-start.3
  3.5 0.0 copy-start.2
  3.5 1.4 %copy-done.2 = s32[192,2048]{1,0:T(8,128)S(1)} copy-done((s32[192,2048]{1,0:T(8,128)S(1)}, s32[192,2048]{1,0:T(8,128)}, u32[]{:S(2)}) %copy-start.2) | copy-done | bytes 1572888
  4.9 0.0 copy-start.3
  4.9 0.0 copy-start.4
  4.9 0.0 copy-start.5
  4.9 0.1 delay.1
  5.0 2.0 %collective-permute-start = (bf16[192,1024]{1,0:T(8,128)(2,1)S(1)}, bf16[192,1024]{1,0:T(8,128)(2,1)S(1)}, u32[]{:S(2)}, u32[]{:S(2)}) collective-permute-start(bf16[192,1024]{1,0:T(8,128)(2,1)S(1)} %get-tuple-element.24), channel_id=1, source_target_pairs={{0,32},{32,0},{64,96},{96,64},{1,33},{33,1},{65,97},{97,65},{2,34}... | collective-permute-start | bytes 1179656 | tf_op jit(solution)/shard_map/ppermute | solution.py:44
  7.0 0.0 copy-done.3
  7.0 0.0 copy-done.4
  7.0 0.0 copy-done.5
  7.0 0.4 band.1
  7.4 1.1 %collective-permute-done.2.refs_2_ = bf16[192,384]{1,0:T(8,128)(2,1)S(1)} collective-permute-done((bf16[192,384]{1,0:T(8,128)(2,1)}, bf16[192,384]{1,0:T(8,128)(2,1)S(1)}, u32[]{:S(2)}, u32[]{:S(2)}) %collective-permute-start.2) | collective-permute-done | bytes 147488 | tf_op jit(solution)/shard_map/ppermute | solution.py:32
  8.5 0.0 collective-permute-done.1.refs_1_
  8.5 2.3 %collective-permute-done.3.refs_3_ = bf16[192,384]{1,0:T(8,128)(2,1)S(1)} collective-permute-done((bf16[192,384]{1,0:T(8,128)(2,1)}, bf16[192,384]{1,0:T(8,128)(2,1)S(1)}, u32[]{:S(2)}, u32[]{:S(2)}) %collective-permute-start.3) | collective-permute-done | bytes 147488 | tf_op jit(solution)/shard_map/ppermute | solution.py:32
  10.8 0.0 copy-done
  10.8 0.0 collective-permute-start.4
  10.8 0.5 collective-permute-start.5
  11.3 0.0 collective-permute-start.6
  11.3 0.5 collective-permute-start.7
  11.8 0.3 collective-permute-done.4.refs_4_
  12.2 0.2 collective-permute-done.5.refs_5_
  12.4 0.3 collective-permute-done.6.refs_6_
  12.7 0.2 collective-permute-done.7.refs_7_
  12.9 0.0 copy-done.1
  12.9 2.2 %window.1.windows = bf16[192,384]{1,0:T(8,128)(2,1)S(1)} custom-call(f32[4]{0:T(128)S(1)} %copy-done.1, bf16[192,384]{1,0:T(8,128)(2,1)S(1)} %copy-done, bf16[192,384]{1,0:T(8,128)(2,1)S(1)} %collective-permute-done.1.refs_1_, bf16[192,384]{1,0:T(8,128)(2,1)S(1)} %collective-permute-done.2.refs_2_, bf16[192,384]{1,0:T(8,128)(2,1)S(1)} %collective-permute-done.3.refs_3_, ...), custom_call_target="tpu_custom_call" | custom-call | flops 1048576 | bytes 65536 | tf_op jit(solution)/shard_map/window/pallas_call | solution.py:255
  15.1 2.2 %collective-permute-start.8 = (bf16[192,384]{1,0:T(8,128)(2,1)S(1)}, bf16[192,384]{1,0:T(8,128)(2,1)S(1)}, u32[]{:S(2)}, u32[]{:S(2)}) collective-permute-start(bf16[192,384]{1,0:T(8,128)(2,1)S(1)} %window.1.windows), channel_id=1, source_target_pairs={{0,32},{32,0},{64,96},{96,64},{1,33},{33,1},{65,97},{97,65},{2,34}... | collective-permute-start | bytes 442376 | tf_op jit(solution)/shard_map/ppermute | solution.py:44
  17.3 5.8 %own_send.1 = (f32[256,512]{1,0:T(8,128)S(1)}, bf16[3,128,12288]{2,1,0:T(8,128)(2,1)S(1)}) custom-call(bf16[192,512]{1,0:T(8,128)(2,1)S(1)} %get-tuple-element.32.delays, bf16[192,384]{1,0:T(8,128)(2,1)S(1)} %window.1.windows), custom_call_target="tpu_custom_call" | custom-call | flops 1048576 | bytes 65536 | tf_op jit(solution)/shard_map/own_send/pallas_call | solution.py:274
  23.1 0.0 collective-permute-done.delays.peer_delays
  23.1 0.0 collective-permute-done.8.windows
  23.1 5.9 %peer_send.1 = (bf16[256,512]{1,0:T(8,128)(2,1)S(1)}, bf16[3,128,12288]{2,1,0:T(8,128)(2,1)S(1)}) custom-call(bf16[192,1024]{1,0:T(8,128)(2,1)S(1)} %collective-permute-done.delays.peer_delays, bf16[192,384]{1,0:T(8,128)(2,1)S(1)} %collective-permute-done.8.windows, f32[256,512]{1,0:T(8,128)S(1)} %get-tuple-element.33.acc), custom_call_target="tpu_custom_call" | custom-call | flops 1048576 | bytes 65536 | tf_op jit(solution)/shard_map/peer_send/pallas_call | solution.py:274
  29.0 2.8 %collective-permute-start.9 = (bf16[256,512]{1,0:T(8,128)(2,1)S(1)}, bf16[256,512]{1,0:T(8,128)(2,1)S(1)}, u32[]{:S(2)}, u32[]{:S(2)}) collective-permute-start(bf16[256,512]{1,0:T(8,128)(2,1)S(1)} %get-tuple-element.39), channel_id=1, source_target_pairs={{0,96},{32,64},{64,32},{96,0},{1,97},{33,65},{65,33},{97,1},{2,98}... | collective-permute-start | bytes 786440 | tf_op jit(solution)/shard_map/ppermute | solution.py:44
  31.8 7.6 %first_keep.1 = (f32[256,256]{1,0:T(8,128)S(1)}, f32[256,256]{1,0:T(8,128)S(1)}) custom-call(bf16[192,512]{1,0:T(8,128)(2,1)S(1)} %get-tuple-element.35.own_delays, bf16[3,128,12288]{2,1,0:T(8,128)(2,1)S(1)} %get-tuple-element.36.own_table, bf16[192,1024]{1,0:T(8,128)(2,1)S(1)} %collective-permute-done.delays.peer_delays, ...), custom_call_target="tpu_custom_call" | custom-call | flops 1048576 | bytes 65536 | tf_op jit(solution)/shard_map/first_keep/pallas_call | solution.py:274
  39.5 0.0 collective-permute-done.9.received
  39.5 0.1 far.1
  39.6 3.1 %collective-permute-start.10 = (bf16[256,256]{1,0:T(8,128)(2,1)S(1)}, bf16[256,256]{1,0:T(8,128)(2,1)S(1)}, u32[]{:S(2)}, u32[]{:S(2)}) collective-permute-start(bf16[256,256]{1,0:T(8,128)(2,1)S(1)} %far.1), channel_id=1, source_target_pairs={{0,24},{8,16},{16,8},{24,0},{1,25},{9,17},{17,9},{25,1},{2,26},{10... | collective-permute-start | bytes 393224 | tf_op jit(solution)/shard_map/ppermute | solution.py:44
  42.7 2.7 %last_keep.1.done = f32[256,256]{1,0:T(8,128)S(1)} custom-call(bf16[192,1024]{1,0:T(8,128)(2,1)S(1)} %collective-permute-done.delays.peer_delays, bf16[3,128,12288]{2,1,0:T(8,128)(2,1)S(1)} %get-tuple-element.34.peer_table, f32[256,256]{1,0:T(8,128)S(1)} %get-tuple-element.40.near, bf16[256,512]{1,0:T(8,128)(2,1)S(1)} %collective-permute-done.9.received), custom_call_target="tpu_custom_call" | custom-call | flops 4294967296 | bytes 65536 | tf_op jit(solution)/shard_map/last_keep/pallas_call | solution.py:274
  45.4 0.7 %collective-permute-done.10.received = bf16[256,256]{1,0:T(8,128)(2,1)S(1)} collective-permute-done((bf16[256,256]{1,0:T(8,128)(2,1)S(1)}, bf16[256,256]{1,0:T(8,128)(2,1)S(1)}, u32[]{:S(2)}, u32[]{:S(2)}) %collective-permute-start.10) | collective-permute-done | bytes 131104 | tf_op jit(solution)/shard_map/ppermute | solution.py:44
  46.1 0.4 collective-permute-start.11
  46.5 4.0 %collective-permute-done.11 = bf16[128,256]{1,0:T(8,128)(2,1)S(1)} collective-permute-done((bf16[128,256]{1,0:T(8,128)(2,1)S(1)}, bf16[128,256]{1,0:T(8,128)(2,1)S(1)}, u32[]{:S(2)}, u32[]{:S(2)}) %collective-permute-start.11) | collective-permute-done | bytes 65568 | tf_op jit(solution)/shard_map/ppermute | solution.py:44
  50.5 0.7 %convert_add_fusion = f32[128,256]{1,0:T(8,128)} fusion(f32[128,256]{1,0:T(8,128)S(1)} %get-tuple-element.41, bf16[128,256]{1,0:T(8,128)(2,1)S(1)} %collective-permute-done.11), kind=kLoop, calls=%fused_computation | loop fusion | flops 65536 | bytes 327680 | tf_op jit(solution)/shard_map/add | solution.py:309
  (1 shorter events, 0.0 us)
Async XLA Ops:
  0.0 10.8 %copy-start = (bf16[192,384]{1,0:T(8,128)(2,1)S(1)}, bf16[192,384]{1,0:T(8,128)(2,1)}, u32[]{:S(2)}) copy-start(bf16[192,384]{1,0:T(8,128)(2,1)} %refs_0_) | copy-start | bytes 442372
  0.0 12.9 %copy-start.1 = (f32[4]{0:T(128)S(1)}, f32[4]{0:T(128)}, u32[]{:S(2)}) copy-start(f32[4]{0:T(128)} %gain.1) | copy-start | bytes 52
  0.0 8.4 %collective-permute-start.2 = (bf16[192,384]{1,0:T(8,128)(2,1)}, bf16[192,384]{1,0:T(8,128)(2,1)S(1)}, u32[]{:S(2)}, u32[]{:S(2)}) collective-permute-start(bf16[192,384]{1,0:T(8,128)(2,1)} %refs_0_), channel_id=1, source_target_pairs={{0,4},{2,6},{4,0},{6,2},{1,5},{3,7},{5,1},{7,3},{8,12},{10,14},{12... | collective-permute-start | bytes 442376 | tf_op jit(solution)/shard_map/ppermute | solution.py:32
  1.4 7.0 %collective-permute-start.1 = (bf16[192,384]{1,0:T(8,128)(2,1)}, bf16[192,384]{1,0:T(8,128)(2,1)S(1)}, u32[]{:S(2)}, u32[]{:S(2)}) collective-permute-start(bf16[192,384]{1,0:T(8,128)(2,1)} %refs_0_), channel_id=1, source_target_pairs={{0,2},{2,4},{4,6},{6,0},{1,3},{3,5},{5,7},{7,1},{8,10},{10,12},{12... | collective-permute-start | bytes 442376 | tf_op jit(solution)/shard_map/ppermute | solution.py:32
  3.5 7.3 %collective-permute-start.3 = (bf16[192,384]{1,0:T(8,128)(2,1)}, bf16[192,384]{1,0:T(8,128)(2,1)S(1)}, u32[]{:S(2)}, u32[]{:S(2)}) collective-permute-start(bf16[192,384]{1,0:T(8,128)(2,1)} %refs_0_), channel_id=1, source_target_pairs={{0,6},{2,0},{4,2},{6,4},{1,7},{3,1},{5,3},{7,5},{8,14},{10,8},{12,... | collective-permute-start | bytes 442376 | tf_op jit(solution)/shard_map/ppermute | solution.py:32
  3.5 1.4 %copy-start.2 = (s32[192,2048]{1,0:T(8,128)S(1)}, s32[192,2048]{1,0:T(8,128)}, u32[]{:S(2)}) copy-start(s32[192,2048]{1,0:T(8,128)} %delays.1) | copy-start | bytes 4718596
  4.9 2.1 %copy-start.3 = (s32[192,8]{0,1:T(8,128)S(1)}, s32[192,8]{0,1:T(8,128)}, u32[]{:S(2)}) copy-start(s32[192,8]{0,1:T(8,128)} %param.9) | copy-start | bytes 18436
  4.9 2.1 %copy-start.4 = (s32[192,8]{0,1:T(8,128)S(1)}, s32[192,8]{0,1:T(8,128)}, u32[]{:S(2)}) copy-start(s32[192,8]{0,1:T(8,128)} %param.11) | copy-start | bytes 18436
  4.9 2.1 %copy-start.5 = (f32[4,64]{1,0:T(4,128)S(1)}, f32[4,64]{1,0:T(4,128)}, u32[]{:S(2)}) copy-start(f32[4,64]{1,0:T(4,128)} %taps.1) | copy-start | bytes 3076
  5.0 18.1 %collective-permute-start = (bf16[192,1024]{1,0:T(8,128)(2,1)S(1)}, bf16[192,1024]{1,0:T(8,128)(2,1)S(1)}, u32[]{:S(2)}, u32[]{:S(2)}) collective-permute-start(bf16[192,1024]{1,0:T(8,128)(2,1)S(1)} %get-tuple-element.24), channel_id=1, source_target_pairs={{0,32},{32,0},{64,96},{96,64},{1,33},{33,1},{65,97},{97,65},{2,34}... | collective-permute-start | bytes 1179656 | tf_op jit(solution)/shard_map/ppermute | solution.py:44
  10.8 1.4 %collective-permute-start.4 = (bf16[192,384]{1,0:T(8,128)(2,1)S(1)}, bf16[192,384]{1,0:T(8,128)(2,1)S(1)}, u32[]{:S(2)}, u32[]{:S(2)}) collective-permute-start(bf16[192,384]{1,0:T(8,128)(2,1)S(1)} %copy-done), channel_id=1, source_target_pairs={{0,1},{1,0},{2,3},{3,2},{4,5},{5,4},{6,7},{7,6},{8,9},{9,8},{10,11... | collective-permute-start | bytes 442376 | tf_op jit(solution)/shard_map/ppermute | solution.py:32
  10.8 1.6 %collective-permute-start.5 = (bf16[192,384]{1,0:T(8,128)(2,1)S(1)}, bf16[192,384]{1,0:T(8,128)(2,1)S(1)}, u32[]{:S(2)}, u32[]{:S(2)}) collective-permute-start(bf16[192,384]{1,0:T(8,128)(2,1)S(1)} %collective-permute-done.1.refs_1_), channel_id=1, source_target_pairs={{0,1},{1,0},{2,3},{3,2},{4,5},{5,4},{6,7},{7,6},{8,9},{9,8},{10,11... | collective-permute-start | bytes 442376 | tf_op jit(solution)/shard_map/ppermute | solution.py:32
  11.3 1.4 %collective-permute-start.6 = (bf16[192,384]{1,0:T(8,128)(2,1)S(1)}, bf16[192,384]{1,0:T(8,128)(2,1)S(1)}, u32[]{:S(2)}, u32[]{:S(2)}) collective-permute-start(bf16[192,384]{1,0:T(8,128)(2,1)S(1)} %collective-permute-done.2.refs_2_), channel_id=1, source_target_pairs={{0,1},{1,0},{2,3},{3,2},{4,5},{5,4},{6,7},{7,6},{8,9},{9,8},{10,11... | collective-permute-start | bytes 442376 | tf_op jit(solution)/shard_map/ppermute | solution.py:32
  11.3 1.6 %collective-permute-start.7 = (bf16[192,384]{1,0:T(8,128)(2,1)S(1)}, bf16[192,384]{1,0:T(8,128)(2,1)S(1)}, u32[]{:S(2)}, u32[]{:S(2)}) collective-permute-start(bf16[192,384]{1,0:T(8,128)(2,1)S(1)} %collective-permute-done.3.refs_3_), channel_id=1, source_target_pairs={{0,1},{1,0},{2,3},{3,2},{4,5},{5,4},{6,7},{7,6},{8,9},{9,8},{10,11... | collective-permute-start | bytes 442376 | tf_op jit(solution)/shard_map/ppermute | solution.py:32
  15.1 8.0 %collective-permute-start.8 = (bf16[192,384]{1,0:T(8,128)(2,1)S(1)}, bf16[192,384]{1,0:T(8,128)(2,1)S(1)}, u32[]{:S(2)}, u32[]{:S(2)}) collective-permute-start(bf16[192,384]{1,0:T(8,128)(2,1)S(1)} %window.1.windows), channel_id=1, source_target_pairs={{0,32},{32,0},{64,96},{96,64},{1,33},{33,1},{65,97},{97,65},{2,34}... | collective-permute-start | bytes 442376 | tf_op jit(solution)/shard_map/ppermute | solution.py:44
  29.0 10.4 %collective-permute-start.9 = (bf16[256,512]{1,0:T(8,128)(2,1)S(1)}, bf16[256,512]{1,0:T(8,128)(2,1)S(1)}, u32[]{:S(2)}, u32[]{:S(2)}) collective-permute-start(bf16[256,512]{1,0:T(8,128)(2,1)S(1)} %get-tuple-element.39), channel_id=1, source_target_pairs={{0,96},{32,64},{64,32},{96,0},{1,97},{33,65},{65,33},{97,1},{2,98}... | collective-permute-start | bytes 786440 | tf_op jit(solution)/shard_map/ppermute | solution.py:44
  39.6 6.5 %collective-permute-start.10 = (bf16[256,256]{1,0:T(8,128)(2,1)S(1)}, bf16[256,256]{1,0:T(8,128)(2,1)S(1)}, u32[]{:S(2)}, u32[]{:S(2)}) collective-permute-start(bf16[256,256]{1,0:T(8,128)(2,1)S(1)} %far.1), channel_id=1, source_target_pairs={{0,24},{8,16},{16,8},{24,0},{1,25},{9,17},{17,9},{25,1},{2,26},{10... | collective-permute-start | bytes 393224 | tf_op jit(solution)/shard_map/ppermute | solution.py:44
  46.1 4.3 %collective-permute-start.11 = (bf16[128,256]{1,0:T(8,128)(2,1)S(1)}, bf16[128,256]{1,0:T(8,128)(2,1)S(1)}, u32[]{:S(2)}, u32[]{:S(2)}) collective-permute-start(bf16[128,256]{1,0:T(8,128)(2,1)S(1)} %get-tuple-element.42), channel_id=1, source_target_pairs={{0,8},{8,0},{16,24},{24,16},{1,9},{9,1},{17,25},{25,17},{2,10},{10... | collective-permute-start | bytes 196616 | tf_op jit(solution)/shard_map/ppermute | solution.py:44

commit v4 on v3

--- a/solution.py
+++ b/solution.py
@@ -10,6 +10,8 @@
 
 TAPS = 64
 HALF = 64
+STEP = 24
+ROWS = 16
 L = 256
 WLEN = 384
 BANDS = 4
@@ -81,39 +83,52 @@
 def window_kernel(gain, *refs):
     chips = 4
     mine, other = refs[:chips], refs[chips : 2 * chips]
-    meta, toeplitz, out, line = refs[2 * chips :]
+    meta, toeplitz, out, line, cut = refs[2 * chips :]
     x, core = lax.axis_index("x"), lax.axis_index("core")
     stations, samp = mine[0].shape
     tiles_in = (2 * chips * samp) // LANE
-    line[:, 0:LANE] = jnp.zeros((stations, LANE), F32)
-    line[:, (tiles_in + 1) * LANE :] = jnp.zeros((stations, LANE), F32)
+    line[:, 0:LANE] = jnp.zeros((stations, LANE), BF16)
+    line[:, (tiles_in + 1) * LANE :] = jnp.zeros((stations, LANE), BF16)
     for k in range(chips):
         chip = lax.rem(x + chips - k, chips)
         for src, c in ((mine, core), (other, 1 - core)):
             at = pl.multiple_of((2 * chip + c) * samp + LANE, LANE)
-            line[:, pl.ds(at, samp)] = src[k][...].astype(F32)
-    first = meta[0]
+            line[:, pl.ds(at, samp)] = src[k][...]
+    keep = WLEN // LANE + 2
+    for r in range(0, stations, ROWS):
+        first = meta[0, r : r + ROWS, :]
+
+        def has(bit):
+            return (first & bit).astype(F32).astype(BF16) != jnp.asarray(0, BF16)
+
+        parts = [line[r : r + ROWS, i * LANE : (i + 1) * LANE] for i in range(tiles_in + 2)]
+        bit = 16
+        while bit:
+            size = min(len(parts), bit - 1 + keep)
+            chosen = has(bit * LANE)
+            parts = [
+                jnp.where(chosen, parts[i + bit], parts[i]) if i + bit < len(parts) else parts[i]
+                for i in range(size)
+            ]
+            bit //= 2
+        span = jnp.concatenate(parts, axis=1)
+        width = span.shape[1]
+        bit = LANE // 2
+        while bit:
+            moved = pltpu.roll(span, width - bit, axis=1)
+            chosen = has(bit)
+            span = jnp.concatenate(
+                [
+                    jnp.where(chosen, moved[:, i : i + LANE], span[:, i : i + LANE])
+                    for i in range(0, width, LANE)
+                ],
+                axis=1,
+            )
+            bit //= 2
+        for j in range(WLEN // LANE):
+            cut[j * stations + r : j * stations + r + ROWS, :] = span[:, j * LANE : j * LANE + 2 * LANE]
     visible = meta[1].astype(F32)
-    parts = [line[:, i * LANE : (i + 1) * LANE] for i in range(tiles_in + 2)]
-    keep = WLEN // LANE + 2
-    bit = 16
-    while bit:
-        size = min(len(parts), bit - 1 + keep)
-        chosen = (first & (bit * LANE)) != 0
-        parts = [
-            jnp.where(chosen, parts[i + bit], parts[i]) if i + bit < len(parts) else parts[i]
-            for i in range(size)
-        ]
-        bit //= 2
-    span = jnp.concatenate(parts, axis=1)
-    width = span.shape[1]
-    bit = LANE // 2
-    while bit:
-        chosen = jnp.concatenate([(first & bit)] * (width // LANE), axis=1) != 0
-        span = jnp.where(chosen, pltpu.roll(span, width - bit, axis=1), span)
-        bit //= 2
-    span = span.astype(BF16)
-    blocks = jnp.concatenate([span[:, j * LANE : j * LANE + 2 * LANE] for j in range(WLEN // LANE)], axis=0)
+    blocks = cut[...]
     filtered = sum(jnp.dot(blocks, toeplitz[p], preferred_element_type=F32) for p in range(3))
     char = sum(gain[b] * jnp.square(filtered[:, b * LANE : (b + 1) * LANE]) for b in range(BANDS))
     char = char.astype(BF16).astype(F32)
@@ -127,31 +142,48 @@
     return jnp.where(delay == jnp.asarray(level, BF16), jnp.asarray(1, BF16), jnp.asarray(0, BF16))
 
 
-def fill_table(windows, table, plain, steps):
+def turn_windows(windows, plain, steps):
     turned = jnp.transpose(windows[...].astype(F32))
     rest = turned[:, LANE:]
     plain[0] = turned[:, 0:LANE]
     plain[1] = jnp.concatenate([rest, pltpu.roll(rest, WLEN - 1, axis=0)], axis=1)
     for i in range(2):
         steps[i] = plain[i, 0 : WLEN - HALF, :] - plain[i, HALF:WLEN, :]
-    for part, (source, first) in enumerate(((steps, 0), (plain, HALF), (steps, HALF))):
-        for tile in range(HALF + HALF // 2):
-            i, d = (0, tile) if tile < HALF else (1, 2 * (tile - HALF))
-            for k in range(2):
-                at = first + k * 2 * HALF + d
-                table[part, k * HALF : (k + 1) * HALF, tile * LANE : (tile + 1) * LANE] = source[
-                    i, at : at + HALF, :
-                ].astype(BF16)
-
-
-def pick_rows(delays, table):
+
+
+def fill_tile(source, first, out, tile):
+    i, d = (0, tile) if tile < HALF else (1, 2 * (tile - HALF))
+    for k in range(2):
+        at = first + k * 2 * HALF + d
+        out[k * HALF : (k + 1) * HALF, tile * LANE : (tile + 1) * LANE] = source[i, at : at + HALF, :].astype(BF16)
+
+
+def pick_rows(delays, table, sources=None):
     shift = jnp.asarray(HALF, BF16)
     low = jnp.where(delays >= shift, delays - shift, delays)
+    tiles = HALF + HALF // 2
+    size = tiles if sources is None else STEP
 
     def product(part, values, base):
         head, rest = values[0:LANE], values[LANE:]
-        rows = [one_hot(head, base + d) for d in range(HALF)] + [one_hot(rest, base + d) for d in range(HALF)]
-        return jnp.dot(table[part], jnp.concatenate(rows, axis=0), preferred_element_type=F32)
+        total = None
+        for begin in range(0, tiles, size):
+            rows = []
+            for tile in range(begin, begin + size):
+                if sources is not None:
+                    fill_tile(*sources[part], table.at[part], tile)
+                if tile < HALF:
+                    rows.append(one_hot(head, base + tile))
+                else:
+                    d = base + 2 * (tile - HALF)
+                    rows += [one_hot(rest, d), one_hot(rest, d + 1)]
+            term = jnp.dot(
+                table[part, :, begin * LANE : (begin + size) * LANE],
+                jnp.concatenate(rows, axis=0),
+                preferred_element_type=F32,
+            )
+            total = term if total is None else total + term
+        return total
 
     first, both, second = product(0, delays, 0), product(1, low, 0), product(2, delays, HALF)
     blocks = []
@@ -161,15 +193,19 @@
     return jnp.concatenate(blocks, axis=0)
 
 
+def shifted_sources(plain, steps):
+    return (steps, 0), (plain, HALF), (steps, HALF)
+
+
 def own_send_kernel(delays, windows, out, table, plain, steps):
-    fill_table(windows, table, plain, steps)
-    out[...] = pick_rows(delays[...], table)
+    turn_windows(windows, plain, steps)
+    out[...] = pick_rows(delays[...], table, shifted_sources(plain, steps))
 
 
 def peer_send_kernel(delays, windows, acc, out, table, plain, steps):
-    fill_table(windows, table, plain, steps)
+    turn_windows(windows, plain, steps)
     half = delays.shape[1] // 2
-    out[...] = (acc[...] + pick_rows(delays[:, 0:half], table)).astype(BF16)
+    out[...] = (acc[...] + pick_rows(delays[:, 0:half], table, shifted_sources(plain, steps))).astype(BF16)
 
 
 def y_blocks(ref, *owners):
@@ -257,7 +293,10 @@
         out_shape=shape((stations, WLEN), BF16),
         in_specs=[smem()] + [vmem()] * 10,
         out_specs=vmem(),
-        scratch_shapes=[pltpu.VMEM((stations, 8 * samp + 2 * LANE), F32)],
+        scratch_shapes=[
+            pltpu.VMEM((stations, 8 * samp + 2 * LANE), BF16),
+            pltpu.VMEM((WLEN // LANE * stations, 2 * LANE), BF16),
+        ],
         compiler_params=params,
         cost_estimate=cost(1 << 20, 1 << 16),
         name="window",

time: 51.3 us -> 51.1 us (level)
  no operation moved by 1% of the time
where the time goes in v4:
time: 51.1 us; the launch traced here: 51 us
  Pallas kernels  24.7 us (48%)
  starting transfers between devices  15 us (29%)
  waiting for transfers between devices  9.1 us (18%)
  local copies, waits for them, and re-layouts  1.43 us (3%)
  other arithmetic  0.67 us (1%)
    pallas_call x6, Pallas kernels, stack(): pl.pallas_call(kernel, out_shape=outs, in_specs=[vmem()] * len(args), out...  22.2 us
    ppermute x5, starting transfers between devices, swap(): return lax.ppermute(value, axis, [(i, peer(i)) for i in range(4)])  10.5 us
    ppermute x5, waiting for transfers between devices, swap(): return lax.ppermute(value, axis, [(i, peer(i)) for i in range(4)])  4.64 us
    ppermute x7, starting transfers between devices, shift_to(): lax.ppermute(value, axis, [(i, (i + by) % length) for i in range(length)])  4.52 us
    ppermute x7, waiting for transfers between devices, shift_to(): lax.ppermute(value, axis, [(i, (i + by) % length) for i in range(length)])  4.45 us
    pallas_call x1, Pallas kernels, on_device(): pl.pallas_call(window_kernel, out_shape=shape((stations, WLEN), BF16), in...  1.97 us
    unnamed x12, local copies, waits for them, and re-layouts  1.43 us
  transfers between devices with their start and end apart: 12, of which 8 were waited for; matrix products, arithmetic and copies ran while one was open for 0% of the time, Pallas kernels for 37%

profile of v4, /device:TPU:6, one launch (start us, length us, event | category | flops | bytes accessed | tf_op | source)
XLA Modules:
  0.0 51.0 jit_solution(12186377289228676583)
XLA Ops:
  0.0 0.0 copy-start
  0.0 0.0 copy-start.1
  0.0 1.4 %collective-permute-start.2 = (bf16[192,384]{1,0:T(8,128)(2,1)}, bf16[192,384]{1,0:T(8,128)(2,1)S(1)}, u32[]{:S(2)}, u32[]{:S(2)}) collective-permute-start(bf16[192,384]{1,0:T(8,128)(2,1)} %refs_0_), channel_id=1, source_target_pairs={{0,4},{2,6},{4,0},{6,2},{1,5},{3,7},{5,1},{7,3},{8,12},{10,14},{12... | collective-permute-start | bytes 442376 | tf_op jit(solution)/shard_map/ppermute | solution.py:34
  1.4 2.1 %collective-permute-start.1 = (bf16[192,384]{1,0:T(8,128)(2,1)}, bf16[192,384]{1,0:T(8,128)(2,1)S(1)}, u32[]{:S(2)}, u32[]{:S(2)}) collective-permute-start(bf16[192,384]{1,0:T(8,128)(2,1)} %refs_0_), channel_id=1, source_target_pairs={{0,2},{2,4},{4,6},{6,0},{1,3},{3,5},{5,7},{7,1},{8,10},{10,12},{12... | collective-permute-start | bytes 442376 | tf_op jit(solution)/shard_map/ppermute | solution.py:34
  3.5 0.0 collective-permute-start.3
  3.5 0.0 copy-start.2
  3.5 1.4 %copy-done.2 = s32[192,2048]{1,0:T(8,128)S(1)} copy-done((s32[192,2048]{1,0:T(8,128)S(1)}, s32[192,2048]{1,0:T(8,128)}, u32[]{:S(2)}) %copy-start.2) | copy-done | bytes 1572888
  4.9 0.0 copy-start.3
  4.9 0.0 copy-start.4
  4.9 0.0 copy-start.5
  4.9 0.1 delay.1
  5.0 2.0 %collective-permute-start = (bf16[192,1024]{1,0:T(8,128)(2,1)S(1)}, bf16[192,1024]{1,0:T(8,128)(2,1)S(1)}, u32[]{:S(2)}, u32[]{:S(2)}) collective-permute-start(bf16[192,1024]{1,0:T(8,128)(2,1)S(1)} %get-tuple-element.24), channel_id=1, source_target_pairs={{0,32},{32,0},{64,96},{96,64},{1,33},{33,1},{65,97},{97,65},{2,34}... | collective-permute-start | bytes 1179656 | tf_op jit(solution)/shard_map/ppermute | solution.py:46
  7.0 0.0 copy-done.3
  7.0 0.0 copy-done.4
  7.0 0.0 copy-done.5
  7.0 0.4 band.1
  7.4 1.1 %collective-permute-done.2.refs_2_ = bf16[192,384]{1,0:T(8,128)(2,1)S(1)} collective-permute-done((bf16[192,384]{1,0:T(8,128)(2,1)}, bf16[192,384]{1,0:T(8,128)(2,1)S(1)}, u32[]{:S(2)}, u32[]{:S(2)}) %collective-permute-start.2) | collective-permute-done | bytes 147488 | tf_op jit(solution)/shard_map/ppermute | solution.py:34
  8.5 0.0 collective-permute-done.1.refs_1_
  8.5 2.3 %collective-permute-done.3.refs_3_ = bf16[192,384]{1,0:T(8,128)(2,1)S(1)} collective-permute-done((bf16[192,384]{1,0:T(8,128)(2,1)}, bf16[192,384]{1,0:T(8,128)(2,1)S(1)}, u32[]{:S(2)}, u32[]{:S(2)}) %collective-permute-start.3) | collective-permute-done | bytes 147488 | tf_op jit(solution)/shard_map/ppermute | solution.py:34
  10.8 0.0 copy-done
  10.8 0.0 collective-permute-start.4
  10.8 0.5 collective-permute-start.5
  11.3 0.0 collective-permute-start.6
  11.3 0.5 collective-permute-start.7
  11.8 0.3 collective-permute-done.4.refs_4_
  12.2 0.2 collective-permute-done.5.refs_5_
  12.4 0.3 collective-permute-done.6.refs_6_
  12.7 0.2 collective-permute-done.7.refs_7_
  12.9 0.0 copy-done.1
  12.9 2.0 %window.1.windows = bf16[192,384]{1,0:T(8,128)(2,1)S(1)} custom-call(f32[4]{0:T(128)S(1)} %copy-done.1, bf16[192,384]{1,0:T(8,128)(2,1)S(1)} %copy-done, bf16[192,384]{1,0:T(8,128)(2,1)S(1)} %collective-permute-done.1.refs_1_, bf16[192,384]{1,0:T(8,128)(2,1)S(1)} %collective-permute-done.2.refs_2_, bf16[192,384]{1,0:T(8,128)(2,1)S(1)} %collective-permute-done.3.refs_3_, ...), custom_call_target="tpu_custom_call" | custom-call | flops 1048576 | bytes 65536 | tf_op jit(solution)/shard_map/window/pallas_call | solution.py:291
  14.9 2.2 %collective-permute-start.8 = (bf16[192,384]{1,0:T(8,128)(2,1)S(1)}, bf16[192,384]{1,0:T(8,128)(2,1)S(1)}, u32[]{:S(2)}, u32[]{:S(2)}) collective-permute-start(bf16[192,384]{1,0:T(8,128)(2,1)S(1)} %window.1.windows), channel_id=1, source_target_pairs={{0,32},{32,0},{64,96},{96,64},{1,33},{33,1},{65,97},{97,65},{2,34}... | collective-permute-start | bytes 442376 | tf_op jit(solution)/shard_map/ppermute | solution.py:46
  17.0 5.9 %own_send.1 = (f32[256,512]{1,0:T(8,128)S(1)}, bf16[3,128,12288]{2,1,0:T(8,128)(2,1)S(1)}) custom-call(bf16[192,512]{1,0:T(8,128)(2,1)S(1)} %get-tuple-element.32.delays, bf16[192,384]{1,0:T(8,128)(2,1)S(1)} %window.1.windows), custom_call_target="tpu_custom_call" | custom-call | flops 1048576 | bytes 65536 | tf_op jit(solution)/shard_map/own_send/pallas_call | solution.py:313
  22.9 0.0 collective-permute-done.delays.peer_delays
  22.9 0.0 collective-permute-done.8.windows
  22.9 5.9 %peer_send.1 = (bf16[256,512]{1,0:T(8,128)(2,1)S(1)}, bf16[3,128,12288]{2,1,0:T(8,128)(2,1)S(1)}) custom-call(bf16[192,1024]{1,0:T(8,128)(2,1)S(1)} %collective-permute-done.delays.peer_delays, bf16[192,384]{1,0:T(8,128)(2,1)S(1)} %collective-permute-done.8.windows, f32[256,512]{1,0:T(8,128)S(1)} %get-tuple-element.33.acc), custom_call_target="tpu_custom_call" | custom-call | flops 1048576 | bytes 65536 | tf_op jit(solution)/shard_map/peer_send/pallas_call | solution.py:313
  28.8 2.8 %collective-permute-start.9 = (bf16[256,512]{1,0:T(8,128)(2,1)S(1)}, bf16[256,512]{1,0:T(8,128)(2,1)S(1)}, u32[]{:S(2)}, u32[]{:S(2)}) collective-permute-start(bf16[256,512]{1,0:T(8,128)(2,1)S(1)} %get-tuple-element.39), channel_id=1, source_target_pairs={{0,96},{32,64},{64,32},{96,0},{1,97},{33,65},{65,33},{97,1},{2,98}... | collective-permute-start | bytes 786440 | tf_op jit(solution)/shard_map/ppermute | solution.py:46
  31.7 7.6 %first_keep.1 = (f32[256,256]{1,0:T(8,128)S(1)}, f32[256,256]{1,0:T(8,128)S(1)}) custom-call(bf16[192,512]{1,0:T(8,128)(2,1)S(1)} %get-tuple-element.35.own_delays, bf16[3,128,12288]{2,1,0:T(8,128)(2,1)S(1)} %get-tuple-element.36.own_table, bf16[192,1024]{1,0:T(8,128)(2,1)S(1)} %collective-permute-done.delays.peer_delays, ...), custom_call_target="tpu_custom_call" | custom-call | flops 1048576 | bytes 65536 | tf_op jit(solution)/shard_map/first_keep/pallas_call | solution.py:313
  39.3 0.0 collective-permute-done.9.received
  39.3 0.1 far.1
  39.4 3.1 %collective-permute-start.10 = (bf16[256,256]{1,0:T(8,128)(2,1)S(1)}, bf16[256,256]{1,0:T(8,128)(2,1)S(1)}, u32[]{:S(2)}, u32[]{:S(2)}) collective-permute-start(bf16[256,256]{1,0:T(8,128)(2,1)S(1)} %far.1), channel_id=1, source_target_pairs={{0,24},{8,16},{16,8},{24,0},{1,25},{9,17},{17,9},{25,1},{2,26},{10... | collective-permute-start | bytes 393224 | tf_op jit(solution)/shard_map/ppermute | solution.py:46
  42.5 2.7 %last_keep.1.done = f32[256,256]{1,0:T(8,128)S(1)} custom-call(bf16[192,1024]{1,0:T(8,128)(2,1)S(1)} %collective-permute-done.delays.peer_delays, bf16[3,128,12288]{2,1,0:T(8,128)(2,1)S(1)} %get-tuple-element.34.peer_table, f32[256,256]{1,0:T(8,128)S(1)} %get-tuple-element.40.near, bf16[256,512]{1,0:T(8,128)(2,1)S(1)} %collective-permute-done.9.received), custom_call_target="tpu_custom_call" | custom-call | flops 4294967296 | bytes 65536 | tf_op jit(solution)/shard_map/last_keep/pallas_call | solution.py:313
  45.2 0.7 %collective-permute-done.10.received = bf16[256,256]{1,0:T(8,128)(2,1)S(1)} collective-permute-done((bf16[256,256]{1,0:T(8,128)(2,1)S(1)}, bf16[256,256]{1,0:T(8,128)(2,1)S(1)}, u32[]{:S(2)}, u32[]{:S(2)}) %collective-permute-start.10) | collective-permute-done | bytes 131104 | tf_op jit(solution)/shard_map/ppermute | solution.py:46
  45.9 0.4 collective-permute-start.11
  46.3 4.0 %collective-permute-done.11 = bf16[128,256]{1,0:T(8,128)(2,1)S(1)} collective-permute-done((bf16[128,256]{1,0:T(8,128)(2,1)S(1)}, bf16[128,256]{1,0:T(8,128)(2,1)S(1)}, u32[]{:S(2)}, u32[]{:S(2)}) %collective-permute-start.11) | collective-permute-done | bytes 65568 | tf_op jit(solution)/shard_map/ppermute | solution.py:46
  50.3 0.7 %convert_add_fusion = f32[128,256]{1,0:T(8,128)} fusion(f32[128,256]{1,0:T(8,128)S(1)} %get-tuple-element.41, bf16[128,256]{1,0:T(8,128)(2,1)S(1)} %collective-permute-done.11), kind=kLoop, calls=%fused_computation | loop fusion | flops 65536 | bytes 327680 | tf_op jit(solution)/shard_map/add | solution.py:348
  (1 shorter events, 0.0 us)
Async XLA Ops:
  0.0 10.8 %copy-start = (bf16[192,384]{1,0:T(8,128)(2,1)S(1)}, bf16[192,384]{1,0:T(8,128)(2,1)}, u32[]{:S(2)}) copy-start(bf16[192,384]{1,0:T(8,128)(2,1)} %refs_0_) | copy-start | bytes 442372
  0.0 12.9 %copy-start.1 = (f32[4]{0:T(128)S(1)}, f32[4]{0:T(128)}, u32[]{:S(2)}) copy-start(f32[4]{0:T(128)} %gain.1) | copy-start | bytes 52
  0.0 8.4 %collective-permute-start.2 = (bf16[192,384]{1,0:T(8,128)(2,1)}, bf16[192,384]{1,0:T(8,128)(2,1)S(1)}, u32[]{:S(2)}, u32[]{:S(2)}) collective-permute-start(bf16[192,384]{1,0:T(8,128)(2,1)} %refs_0_), channel_id=1, source_target_pairs={{0,4},{2,6},{4,0},{6,2},{1,5},{3,7},{5,1},{7,3},{8,12},{10,14},{12... | collective-permute-start | bytes 442376 | tf_op jit(solution)/shard_map/ppermute | solution.py:34
  1.4 7.0 %collective-permute-start.1 = (bf16[192,384]{1,0:T(8,128)(2,1)}, bf16[192,384]{1,0:T(8,128)(2,1)S(1)}, u32[]{:S(2)}, u32[]{:S(2)}) collective-permute-start(bf16[192,384]{1,0:T(8,128)(2,1)} %refs_0_), channel_id=1, source_target_pairs={{0,2},{2,4},{4,6},{6,0},{1,3},{3,5},{5,7},{7,1},{8,10},{10,12},{12... | collective-permute-start | bytes 442376 | tf_op jit(solution)/shard_map/ppermute | solution.py:34
  3.5 7.3 %collective-permute-start.3 = (bf16[192,384]{1,0:T(8,128)(2,1)}, bf16[192,384]{1,0:T(8,128)(2,1)S(1)}, u32[]{:S(2)}, u32[]{:S(2)}) collective-permute-start(bf16[192,384]{1,0:T(8,128)(2,1)} %refs_0_), channel_id=1, source_target_pairs={{0,6},{2,0},{4,2},{6,4},{1,7},{3,1},{5,3},{7,5},{8,14},{10,8},{12,... | collective-permute-start | bytes 442376 | tf_op jit(solution)/shard_map/ppermute | solution.py:34
  3.5 1.4 %copy-start.2 = (s32[192,2048]{1,0:T(8,128)S(1)}, s32[192,2048]{1,0:T(8,128)}, u32[]{:S(2)}) copy-start(s32[192,2048]{1,0:T(8,128)} %delays.1) | copy-start | bytes 4718596
  4.9 2.1 %copy-start.3 = (s32[192,8]{0,1:T(8,128)S(1)}, s32[192,8]{0,1:T(8,128)}, u32[]{:S(2)}) copy-start(s32[192,8]{0,1:T(8,128)} %param.9) | copy-start | bytes 18436
  4.9 2.1 %copy-start.4 = (s32[192,8]{0,1:T(8,128)S(1)}, s32[192,8]{0,1:T(8,128)}, u32[]{:S(2)}) copy-start(s32[192,8]{0,1:T(8,128)} %param.11) | copy-start | bytes 18436
  4.9 2.1 %copy-start.5 = (f32[4,64]{1,0:T(4,128)S(1)}, f32[4,64]{1,0:T(4,128)}, u32[]{:S(2)}) copy-start(f32[4,64]{1,0:T(4,128)} %taps.1) | copy-start | bytes 3076
  5.0 17.9 %collective-permute-start = (bf16[192,1024]{1,0:T(8,128)(2,1)S(1)}, bf16[192,1024]{1,0:T(8,128)(2,1)S(1)}, u32[]{:S(2)}, u32[]{:S(2)}) collective-permute-start(bf16[192,1024]{1,0:T(8,128)(2,1)S(1)} %get-tuple-element.24), channel_id=1, source_target_pairs={{0,32},{32,0},{64,96},{96,64},{1,33},{33,1},{65,97},{97,65},{2,34}... | collective-permute-start | bytes 1179656 | tf_op jit(solution)/shard_map/ppermute | solution.py:46
  10.8 1.4 %collective-permute-start.4 = (bf16[192,384]{1,0:T(8,128)(2,1)S(1)}, bf16[192,384]{1,0:T(8,128)(2,1)S(1)}, u32[]{:S(2)}, u32[]{:S(2)}) collective-permute-start(bf16[192,384]{1,0:T(8,128)(2,1)S(1)} %copy-done), channel_id=1, source_target_pairs={{0,1},{1,0},{2,3},{3,2},{4,5},{5,4},{6,7},{7,6},{8,9},{9,8},{10,11... | collective-permute-start | bytes 442376 | tf_op jit(solution)/shard_map/ppermute | solution.py:34
  10.8 1.6 %collective-permute-start.5 = (bf16[192,384]{1,0:T(8,128)(2,1)S(1)}, bf16[192,384]{1,0:T(8,128)(2,1)S(1)}, u32[]{:S(2)}, u32[]{:S(2)}) collective-permute-start(bf16[192,384]{1,0:T(8,128)(2,1)S(1)} %collective-permute-done.1.refs_1_), channel_id=1, source_target_pairs={{0,1},{1,0},{2,3},{3,2},{4,5},{5,4},{6,7},{7,6},{8,9},{9,8},{10,11... | collective-permute-start | bytes 442376 | tf_op jit(solution)/shard_map/ppermute | solution.py:34
  11.3 1.4 %collective-permute-start.6 = (bf16[192,384]{1,0:T(8,128)(2,1)S(1)}, bf16[192,384]{1,0:T(8,128)(2,1)S(1)}, u32[]{:S(2)}, u32[]{:S(2)}) collective-permute-start(bf16[192,384]{1,0:T(8,128)(2,1)S(1)} %collective-permute-done.2.refs_2_), channel_id=1, source_target_pairs={{0,1},{1,0},{2,3},{3,2},{4,5},{5,4},{6,7},{7,6},{8,9},{9,8},{10,11... | collective-permute-start | bytes 442376 | tf_op jit(solution)/shard_map/ppermute | solution.py:34
  11.3 1.6 %collective-permute-start.7 = (bf16[192,384]{1,0:T(8,128)(2,1)S(1)}, bf16[192,384]{1,0:T(8,128)(2,1)S(1)}, u32[]{:S(2)}, u32[]{:S(2)}) collective-permute-start(bf16[192,384]{1,0:T(8,128)(2,1)S(1)} %collective-permute-done.3.refs_3_), channel_id=1, source_target_pairs={{0,1},{1,0},{2,3},{3,2},{4,5},{5,4},{6,7},{7,6},{8,9},{9,8},{10,11... | collective-permute-start | bytes 442376 | tf_op jit(solution)/shard_map/ppermute | solution.py:34
  14.9 8.1 %collective-permute-start.8 = (bf16[192,384]{1,0:T(8,128)(2,1)S(1)}, bf16[192,384]{1,0:T(8,128)(2,1)S(1)}, u32[]{:S(2)}, u32[]{:S(2)}) collective-permute-start(bf16[192,384]{1,0:T(8,128)(2,1)S(1)} %window.1.windows), channel_id=1, source_target_pairs={{0,32},{32,0},{64,96},{96,64},{1,33},{33,1},{65,97},{97,65},{2,34}... | collective-permute-start | bytes 442376 | tf_op jit(solution)/shard_map/ppermute | solution.py:46
  28.8 10.5 %collective-permute-start.9 = (bf16[256,512]{1,0:T(8,128)(2,1)S(1)}, bf16[256,512]{1,0:T(8,128)(2,1)S(1)}, u32[]{:S(2)}, u32[]{:S(2)}) collective-permute-start(bf16[256,512]{1,0:T(8,128)(2,1)S(1)} %get-tuple-element.39), channel_id=1, source_target_pairs={{0,96},{32,64},{64,32},{96,0},{1,97},{33,65},{65,33},{97,1},{2,98}... | collective-permute-start | bytes 786440 | tf_op jit(solution)/shard_map/ppermute | solution.py:46
  39.4 6.5 %collective-permute-start.10 = (bf16[256,256]{1,0:T(8,128)(2,1)S(1)}, bf16[256,256]{1,0:T(8,128)(2,1)S(1)}, u32[]{:S(2)}, u32[]{:S(2)}) collective-permute-start(bf16[256,256]{1,0:T(8,128)(2,1)S(1)} %far.1), channel_id=1, source_target_pairs={{0,24},{8,16},{16,8},{24,0},{1,25},{9,17},{17,9},{25,1},{2,26},{10... | collective-permute-start | bytes 393224 | tf_op jit(solution)/shard_map/ppermute | solution.py:46
  45.9 4.3 %collective-permute-start.11 = (bf16[128,256]{1,0:T(8,128)(2,1)S(1)}, bf16[128,256]{1,0:T(8,128)(2,1)S(1)}, u32[]{:S(2)}, u32[]{:S(2)}) collective-permute-start(bf16[128,256]{1,0:T(8,128)(2,1)S(1)} %get-tuple-element.42), channel_id=1, source_target_pairs={{0,8},{8,0},{16,24},{24,16},{1,9},{9,1},{17,25},{25,17},{2,10},{10... | collective-permute-start | bytes 196616 | tf_op jit(solution)/shard_map/ppermute | solution.py:46

commit v5 on v4

--- a/solution.py
+++ b/solution.py
@@ -83,7 +83,7 @@
 def window_kernel(gain, *refs):
     chips = 4
     mine, other = refs[:chips], refs[chips : 2 * chips]
-    meta, toeplitz, out, line, cut = refs[2 * chips :]
+    meta, toeplitz, out, turned, line, cut = refs[2 * chips :]
     x, core = lax.axis_index("x"), lax.axis_index("core")
     stations, samp = mine[0].shape
     tiles_in = (2 * chips * samp) // LANE
@@ -134,19 +134,23 @@
     char = char.astype(BF16).astype(F32)
     pieces = [char[j * stations : (j + 1) * stations] for j in range(WLEN // LANE)]
     mean = jnp.sum(sum(pieces), axis=1, keepdims=True) / WLEN
-    for j, piece in enumerate(pieces):
-        out[:, j * LANE : (j + 1) * LANE] = ((piece - mean) * visible).astype(BF16)
+    centred = jnp.concatenate([(piece - mean) * visible for piece in pieces], axis=1).astype(BF16)
+    out[...] = centred
+    turn_rows(centred, turned)
 
 
 def one_hot(delay, level):
     return jnp.where(delay == jnp.asarray(level, BF16), jnp.asarray(1, BF16), jnp.asarray(0, BF16))
 
 
-def turn_windows(windows, plain, steps):
-    turned = jnp.transpose(windows[...].astype(F32))
+def turn_rows(windows, plain):
+    turned = jnp.transpose(windows.astype(F32))
     rest = turned[:, LANE:]
     plain[0] = turned[:, 0:LANE]
     plain[1] = jnp.concatenate([rest, pltpu.roll(rest, WLEN - 1, axis=0)], axis=1)
+
+
+def difference(plain, steps):
     for i in range(2):
         steps[i] = plain[i, 0 : WLEN - HALF, :] - plain[i, HALF:WLEN, :]
 
@@ -197,13 +201,14 @@
     return (steps, 0), (plain, HALF), (steps, HALF)
 
 
-def own_send_kernel(delays, windows, out, table, plain, steps):
-    turn_windows(windows, plain, steps)
+def own_send_kernel(delays, plain, out, table, steps):
+    difference(plain, steps)
     out[...] = pick_rows(delays[...], table, shifted_sources(plain, steps))
 
 
 def peer_send_kernel(delays, windows, acc, out, table, plain, steps):
-    turn_windows(windows, plain, steps)
+    turn_rows(windows[...], plain)
+    difference(plain, steps)
     half = delays.shape[1] // 2
     out[...] = (acc[...] + pick_rows(delays[:, 0:half], table, shifted_sources(plain, steps))).astype(BF16)
 
@@ -288,11 +293,11 @@
     near, toeplitz, _ = lax.optimization_barrier((near, toeplitz, peer_both))
     other = [shift_to(block, "core", 1) for block in near]
 
-    windows = pl.pallas_call(
+    windows, own_turned = pl.pallas_call(
         window_kernel,
-        out_shape=shape((stations, WLEN), BF16),
+        out_shape=[shape((stations, WLEN), BF16), shape((2, WLEN, LANE), F32)],
         in_specs=[smem()] + [vmem()] * 10,
-        out_specs=vmem(),
+        out_specs=[vmem()] * 2,
         scratch_shapes=[
             pltpu.VMEM((stations, 8 * samp + 2 * LANE), BF16),
             pltpu.VMEM((WLEN // LANE * stations, 2 * LANE), BF16),
@@ -321,7 +326,7 @@
             name=name,
         )(*args)
 
-    acc, own_table = stack(own_send_kernel, "own_send", [whole, table], [own_send, windows], turned)
+    acc, own_table = stack(own_send_kernel, "own_send", [whole, table], [own_send, own_turned], turned[1:])
     away, peer_table = stack(
         peer_send_kernel, "peer_send", [shape((L, piece), BF16), table], [peer_rows, peer_windows, acc], turned
     )

time: 51.1 us -> 51 us (level)
  transfers between devices with their start and end apart: 12 -> 12, of which waited for: 8 -> 8; matrix products, arithmetic and copies ran while one was open for 0% -> 0% of each run, Pallas kernels for 37% -> 36%
where the time goes in v5:
time: 51 us; the launch traced here: 50.9 us
  Pallas kernels  24.6 us (48%)
  starting transfers between devices  15 us (29%)
  waiting for transfers between devices  9.09 us (18%)
  local copies, waits for them, and re-layouts  1.43 us (3%)
  other arithmetic  0.67 us (1%)
    pallas_call x6, Pallas kernels, stack(): pl.pallas_call(kernel, out_shape=outs, in_specs=[vmem()] * len(args), out...  22 us
    ppermute x5, starting transfers between devices, swap(): return lax.ppermute(value, axis, [(i, peer(i)) for i in range(4)])  10.5 us
    ppermute x5, waiting for transfers between devices, swap(): return lax.ppermute(value, axis, [(i, peer(i)) for i in range(4)])  4.63 us
    ppermute x7, starting transfers between devices, shift_to(): lax.ppermute(value, axis, [(i, (i + by) % length) for i in range(length)])  4.52 us
    ppermute x7, waiting for transfers between devices, shift_to(): lax.ppermute(value, axis, [(i, (i + by) % length) for i in range(length)])  4.45 us
    pallas_call x1, Pallas kernels, on_device(): pl.pallas_call(window_kernel, out_shape=[shape((stations, WLEN), BF16), s...  2.14 us
    unnamed x12, local copies, waits for them, and re-layouts  1.43 us
  transfers between devices with their start and end apart: 12, of which 8 were waited for; matrix products, arithmetic and copies ran while one was open for 0% of the time, Pallas kernels for 36%

profile of v5, /device:TPU:6, one launch (start us, length us, event | category | flops | bytes accessed | tf_op | source)
XLA Modules:
  0.0 50.9 jit_solution(1901513968041221769)
XLA Ops:
  0.0 0.0 copy-start
  0.0 0.0 copy-start.1
  0.0 1.4 %collective-permute-start.2 = (bf16[192,384]{1,0:T(8,128)(2,1)}, bf16[192,384]{1,0:T(8,128)(2,1)S(1)}, u32[]{:S(2)}, u32[]{:S(2)}) collective-permute-start(bf16[192,384]{1,0:T(8,128)(2,1)} %refs_0_), channel_id=1, source_target_pairs={{0,4},{2,6},{4,0},{6,2},{1,5},{3,7},{5,1},{7,3},{8,12},{10,14},{12... | collective-permute-start | bytes 442376 | tf_op jit(solution)/shard_map/ppermute | solution.py:34
  1.4 2.1 %collective-permute-start.1 = (bf16[192,384]{1,0:T(8,128)(2,1)}, bf16[192,384]{1,0:T(8,128)(2,1)S(1)}, u32[]{:S(2)}, u32[]{:S(2)}) collective-permute-start(bf16[192,384]{1,0:T(8,128)(2,1)} %refs_0_), channel_id=1, source_target_pairs={{0,2},{2,4},{4,6},{6,0},{1,3},{3,5},{5,7},{7,1},{8,10},{10,12},{12... | collective-permute-start | bytes 442376 | tf_op jit(solution)/shard_map/ppermute | solution.py:34
  3.5 0.0 collective-permute-start.3
  3.5 0.0 copy-start.2
  3.5 1.4 %copy-done.2 = s32[192,2048]{1,0:T(8,128)S(1)} copy-done((s32[192,2048]{1,0:T(8,128)S(1)}, s32[192,2048]{1,0:T(8,128)}, u32[]{:S(2)}) %copy-start.2) | copy-done | bytes 1572888
  4.9 0.0 copy-start.3
  4.9 0.0 copy-start.4
  4.9 0.0 copy-start.5
  4.9 0.1 delay.1
  5.0 2.0 %collective-permute-start = (bf16[192,1024]{1,0:T(8,128)(2,1)S(1)}, bf16[192,1024]{1,0:T(8,128)(2,1)S(1)}, u32[]{:S(2)}, u32[]{:S(2)}) collective-permute-start(bf16[192,1024]{1,0:T(8,128)(2,1)S(1)} %get-tuple-element.26), channel_id=1, source_target_pairs={{0,32},{32,0},{64,96},{96,64},{1,33},{33,1},{65,97},{97,65},{2,34}... | collective-permute-start | bytes 1179656 | tf_op jit(solution)/shard_map/ppermute | solution.py:46
  7.0 0.0 copy-done.3
  7.0 0.0 copy-done.4
  7.0 0.0 copy-done.5
  7.0 0.4 band.1
  7.4 1.1 %collective-permute-done.2.refs_2_ = bf16[192,384]{1,0:T(8,128)(2,1)S(1)} collective-permute-done((bf16[192,384]{1,0:T(8,128)(2,1)}, bf16[192,384]{1,0:T(8,128)(2,1)S(1)}, u32[]{:S(2)}, u32[]{:S(2)}) %collective-permute-start.2) | collective-permute-done | bytes 147488 | tf_op jit(solution)/shard_map/ppermute | solution.py:34
  8.5 0.0 collective-permute-done.1.refs_1_
  8.5 2.3 %collective-permute-done.3.refs_3_ = bf16[192,384]{1,0:T(8,128)(2,1)S(1)} collective-permute-done((bf16[192,384]{1,0:T(8,128)(2,1)}, bf16[192,384]{1,0:T(8,128)(2,1)S(1)}, u32[]{:S(2)}, u32[]{:S(2)}) %collective-permute-start.3) | collective-permute-done | bytes 147488 | tf_op jit(solution)/shard_map/ppermute | solution.py:34
  10.8 0.0 copy-done
  10.8 0.0 collective-permute-start.4
  10.8 0.5 collective-permute-start.5
  11.3 0.0 collective-permute-start.6
  11.3 0.5 collective-permute-start.7
  11.8 0.3 collective-permute-done.4.refs_4_
  12.2 0.2 collective-permute-done.5.refs_5_
  12.4 0.3 collective-permute-done.6.refs_6_
  12.7 0.2 collective-permute-done.7.refs_7_
  12.9 0.0 copy-done.1
  12.9 2.1 %window.1 = (bf16[192,384]{1,0:T(8,128)(2,1)S(1)}, f32[2,384,128]{2,1,0:T(8,128)S(1)}) custom-call(f32[4]{0:T(128)S(1)} %copy-done.1, bf16[192,384]{1,0:T(8,128)(2,1)S(1)} %copy-done, bf16[192,384]{1,0:T(8,128)(2,1)S(1)} %collective-permute-done.1.refs_1_, bf16[192,384]{1,0:T(8,128)(2,1)S(1)} %collective-permute-done.2.refs_2_, ...), custom_call_target="tpu_custom_call" | custom-call | flops 1048576 | bytes 65536 | tf_op jit(solution)/shard_map/window/pallas_call | solution.py:296
  15.0 2.2 %collective-permute-start.8 = (bf16[192,384]{1,0:T(8,128)(2,1)S(1)}, bf16[192,384]{1,0:T(8,128)(2,1)S(1)}, u32[]{:S(2)}, u32[]{:S(2)}) collective-permute-start(bf16[192,384]{1,0:T(8,128)(2,1)S(1)} %get-tuple-element.34), channel_id=1, source_target_pairs={{0,32},{32,0},{64,96},{96,64},{1,33},{33,1},{65,97},{97,65},{2,34}... | collective-permute-start | bytes 442376 | tf_op jit(solution)/shard_map/ppermute | solution.py:46
  17.2 5.6 %own_send.1 = (f32[256,512]{1,0:T(8,128)S(1)}, bf16[3,128,12288]{2,1,0:T(8,128)(2,1)S(1)}) custom-call(bf16[192,512]{1,0:T(8,128)(2,1)S(1)} %get-tuple-element.35.delays, f32[2,384,128]{2,1,0:T(8,128)S(1)} %get-tuple-element.36.plain), custom_call_target="tpu_custom_call" | custom-call | flops 1048576 | bytes 65536 | tf_op jit(solution)/shard_map/own_send/pallas_call | solution.py:318
  22.8 0.0 collective-permute-done.delays.peer_delays
  22.8 0.0 collective-permute-done.8.windows
  22.9 5.9 %peer_send.1 = (bf16[256,512]{1,0:T(8,128)(2,1)S(1)}, bf16[3,128,12288]{2,1,0:T(8,128)(2,1)S(1)}) custom-call(bf16[192,1024]{1,0:T(8,128)(2,1)S(1)} %collective-permute-done.delays.peer_delays, bf16[192,384]{1,0:T(8,128)(2,1)S(1)} %collective-permute-done.8.windows, f32[256,512]{1,0:T(8,128)S(1)} %get-tuple-element.37.acc), custom_call_target="tpu_custom_call" | custom-call | flops 1048576 | bytes 65536 | tf_op jit(solution)/shard_map/peer_send/pallas_call | solution.py:318
  28.7 2.8 %collective-permute-start.9 = (bf16[256,512]{1,0:T(8,128)(2,1)S(1)}, bf16[256,512]{1,0:T(8,128)(2,1)S(1)}, u32[]{:S(2)}, u32[]{:S(2)}) collective-permute-start(bf16[256,512]{1,0:T(8,128)(2,1)S(1)} %get-tuple-element.43), channel_id=1, source_target_pairs={{0,96},{32,64},{64,32},{96,0},{1,97},{33,65},{65,33},{97,1},{2,98}... | collective-permute-start | bytes 786440 | tf_op jit(solution)/shard_map/ppermute | solution.py:46
  31.6 7.6 %first_keep.1 = (f32[256,256]{1,0:T(8,128)S(1)}, f32[256,256]{1,0:T(8,128)S(1)}) custom-call(bf16[192,512]{1,0:T(8,128)(2,1)S(1)} %get-tuple-element.39.own_delays, bf16[3,128,12288]{2,1,0:T(8,128)(2,1)S(1)} %get-tuple-element.40.own_table, bf16[192,1024]{1,0:T(8,128)(2,1)S(1)} %collective-permute-done.delays.peer_delays, ...), custom_call_target="tpu_custom_call" | custom-call | flops 1048576 | bytes 65536 | tf_op jit(solution)/shard_map/first_keep/pallas_call | solution.py:318
  39.2 0.0 collective-permute-done.9.received
  39.2 0.1 far.1
  39.3 3.1 %collective-permute-start.10 = (bf16[256,256]{1,0:T(8,128)(2,1)S(1)}, bf16[256,256]{1,0:T(8,128)(2,1)S(1)}, u32[]{:S(2)}, u32[]{:S(2)}) collective-permute-start(bf16[256,256]{1,0:T(8,128)(2,1)S(1)} %far.1), channel_id=1, source_target_pairs={{0,24},{8,16},{16,8},{24,0},{1,25},{9,17},{17,9},{25,1},{2,26},{10... | collective-permute-start | bytes 393224 | tf_op jit(solution)/shard_map/ppermute | solution.py:46
  42.4 2.7 %last_keep.1.done = f32[256,256]{1,0:T(8,128)S(1)} custom-call(bf16[192,1024]{1,0:T(8,128)(2,1)S(1)} %collective-permute-done.delays.peer_delays, bf16[3,128,12288]{2,1,0:T(8,128)(2,1)S(1)} %get-tuple-element.38.peer_table, f32[256,256]{1,0:T(8,128)S(1)} %get-tuple-element.44.near, bf16[256,512]{1,0:T(8,128)(2,1)S(1)} %collective-permute-done.9.received), custom_call_target="tpu_custom_call" | custom-call | flops 4294967296 | bytes 65536 | tf_op jit(solution)/shard_map/last_keep/pallas_call | solution.py:318
  45.1 0.7 %collective-permute-done.10.received = bf16[256,256]{1,0:T(8,128)(2,1)S(1)} collective-permute-done((bf16[256,256]{1,0:T(8,128)(2,1)S(1)}, bf16[256,256]{1,0:T(8,128)(2,1)S(1)}, u32[]{:S(2)}, u32[]{:S(2)}) %collective-permute-start.10) | collective-permute-done | bytes 131104 | tf_op jit(solution)/shard_map/ppermute | solution.py:46
  45.8 0.4 collective-permute-start.11
  46.2 3.9 %collective-permute-done.11 = bf16[128,256]{1,0:T(8,128)(2,1)S(1)} collective-permute-done((bf16[128,256]{1,0:T(8,128)(2,1)S(1)}, bf16[128,256]{1,0:T(8,128)(2,1)S(1)}, u32[]{:S(2)}, u32[]{:S(2)}) %collective-permute-start.11) | collective-permute-done | bytes 65568 | tf_op jit(solution)/shard_map/ppermute | solution.py:46
  50.2 0.7 %convert_add_fusion = f32[128,256]{1,0:T(8,128)} fusion(f32[128,256]{1,0:T(8,128)S(1)} %get-tuple-element.45, bf16[128,256]{1,0:T(8,128)(2,1)S(1)} %collective-permute-done.11), kind=kLoop, calls=%fused_computation | loop fusion | flops 65536 | bytes 327680 | tf_op jit(solution)/shard_map/add | solution.py:353
  (1 shorter events, 0.0 us)
Async XLA Ops:
  0.0 10.8 %copy-start = (bf16[192,384]{1,0:T(8,128)(2,1)S(1)}, bf16[192,384]{1,0:T(8,128)(2,1)}, u32[]{:S(2)}) copy-start(bf16[192,384]{1,0:T(8,128)(2,1)} %refs_0_) | copy-start | bytes 442372
  0.0 12.9 %copy-start.1 = (f32[4]{0:T(128)S(1)}, f32[4]{0:T(128)}, u32[]{:S(2)}) copy-start(f32[4]{0:T(128)} %gain.1) | copy-start | bytes 52
  0.0 8.4 %collective-permute-start.2 = (bf16[192,384]{1,0:T(8,128)(2,1)}, bf16[192,384]{1,0:T(8,128)(2,1)S(1)}, u32[]{:S(2)}, u32[]{:S(2)}) collective-permute-start(bf16[192,384]{1,0:T(8,128)(2,1)} %refs_0_), channel_id=1, source_target_pairs={{0,4},{2,6},{4,0},{6,2},{1,5},{3,7},{5,1},{7,3},{8,12},{10,14},{12... | collective-permute-start | bytes 442376 | tf_op jit(solution)/shard_map/ppermute | solution.py:34
  1.4 7.0 %collective-permute-start.1 = (bf16[192,384]{1,0:T(8,128)(2,1)}, bf16[192,384]{1,0:T(8,128)(2,1)S(1)}, u32[]{:S(2)}, u32[]{:S(2)}) collective-permute-start(bf16[192,384]{1,0:T(8,128)(2,1)} %refs_0_), channel_id=1, source_target_pairs={{0,2},{2,4},{4,6},{6,0},{1,3},{3,5},{5,7},{7,1},{8,10},{10,12},{12... | collective-permute-start | bytes 442376 | tf_op jit(solution)/shard_map/ppermute | solution.py:34
  3.5 7.3 %collective-permute-start.3 = (bf16[192,384]{1,0:T(8,128)(2,1)}, bf16[192,384]{1,0:T(8,128)(2,1)S(1)}, u32[]{:S(2)}, u32[]{:S(2)}) collective-permute-start(bf16[192,384]{1,0:T(8,128)(2,1)} %refs_0_), channel_id=1, source_target_pairs={{0,6},{2,0},{4,2},{6,4},{1,7},{3,1},{5,3},{7,5},{8,14},{10,8},{12,... | collective-permute-start | bytes 442376 | tf_op jit(solution)/shard_map/ppermute | solution.py:34
  3.5 1.4 %copy-start.2 = (s32[192,2048]{1,0:T(8,128)S(1)}, s32[192,2048]{1,0:T(8,128)}, u32[]{:S(2)}) copy-start(s32[192,2048]{1,0:T(8,128)} %delays.1) | copy-start | bytes 4718596
  4.9 2.1 %copy-start.3 = (s32[192,8]{0,1:T(8,128)S(1)}, s32[192,8]{0,1:T(8,128)}, u32[]{:S(2)}) copy-start(s32[192,8]{0,1:T(8,128)} %param.9) | copy-start | bytes 18436
  4.9 2.1 %copy-start.4 = (s32[192,8]{0,1:T(8,128)S(1)}, s32[192,8]{0,1:T(8,128)}, u32[]{:S(2)}) copy-start(s32[192,8]{0,1:T(8,128)} %param.11) | copy-start | bytes 18436
  4.9 2.1 %copy-start.5 = (f32[4,64]{1,0:T(4,128)S(1)}, f32[4,64]{1,0:T(4,128)}, u32[]{:S(2)}) copy-start(f32[4,64]{1,0:T(4,128)} %taps.1) | copy-start | bytes 3076
  5.0 17.8 %collective-permute-start = (bf16[192,1024]{1,0:T(8,128)(2,1)S(1)}, bf16[192,1024]{1,0:T(8,128)(2,1)S(1)}, u32[]{:S(2)}, u32[]{:S(2)}) collective-permute-start(bf16[192,1024]{1,0:T(8,128)(2,1)S(1)} %get-tuple-element.26), channel_id=1, source_target_pairs={{0,32},{32,0},{64,96},{96,64},{1,33},{33,1},{65,97},{97,65},{2,34}... | collective-permute-start | bytes 1179656 | tf_op jit(solution)/shard_map/ppermute | solution.py:46
  10.8 1.4 %collective-permute-start.4 = (bf16[192,384]{1,0:T(8,128)(2,1)S(1)}, bf16[192,384]{1,0:T(8,128)(2,1)S(1)}, u32[]{:S(2)}, u32[]{:S(2)}) collective-permute-start(bf16[192,384]{1,0:T(8,128)(2,1)S(1)} %copy-done), channel_id=1, source_target_pairs={{0,1},{1,0},{2,3},{3,2},{4,5},{5,4},{6,7},{7,6},{8,9},{9,8},{10,11... | collective-permute-start | bytes 442376 | tf_op jit(solution)/shard_map/ppermute | solution.py:34
  10.8 1.6 %collective-permute-start.5 = (bf16[192,384]{1,0:T(8,128)(2,1)S(1)}, bf16[192,384]{1,0:T(8,128)(2,1)S(1)}, u32[]{:S(2)}, u32[]{:S(2)}) collective-permute-start(bf16[192,384]{1,0:T(8,128)(2,1)S(1)} %collective-permute-done.1.refs_1_), channel_id=1, source_target_pairs={{0,1},{1,0},{2,3},{3,2},{4,5},{5,4},{6,7},{7,6},{8,9},{9,8},{10,11... | collective-permute-start | bytes 442376 | tf_op jit(solution)/shard_map/ppermute | solution.py:34
  11.3 1.4 %collective-permute-start.6 = (bf16[192,384]{1,0:T(8,128)(2,1)S(1)}, bf16[192,384]{1,0:T(8,128)(2,1)S(1)}, u32[]{:S(2)}, u32[]{:S(2)}) collective-permute-start(bf16[192,384]{1,0:T(8,128)(2,1)S(1)} %collective-permute-done.2.refs_2_), channel_id=1, source_target_pairs={{0,1},{1,0},{2,3},{3,2},{4,5},{5,4},{6,7},{7,6},{8,9},{9,8},{10,11... | collective-permute-start | bytes 442376 | tf_op jit(solution)/shard_map/ppermute | solution.py:34
  11.3 1.6 %collective-permute-start.7 = (bf16[192,384]{1,0:T(8,128)(2,1)S(1)}, bf16[192,384]{1,0:T(8,128)(2,1)S(1)}, u32[]{:S(2)}, u32[]{:S(2)}) collective-permute-start(bf16[192,384]{1,0:T(8,128)(2,1)S(1)} %collective-permute-done.3.refs_3_), channel_id=1, source_target_pairs={{0,1},{1,0},{2,3},{3,2},{4,5},{5,4},{6,7},{7,6},{8,9},{9,8},{10,11... | collective-permute-start | bytes 442376 | tf_op jit(solution)/shard_map/ppermute | solution.py:34
  15.0 7.8 %collective-permute-start.8 = (bf16[192,384]{1,0:T(8,128)(2,1)S(1)}, bf16[192,384]{1,0:T(8,128)(2,1)S(1)}, u32[]{:S(2)}, u32[]{:S(2)}) collective-permute-start(bf16[192,384]{1,0:T(8,128)(2,1)S(1)} %get-tuple-element.34), channel_id=1, source_target_pairs={{0,32},{32,0},{64,96},{96,64},{1,33},{33,1},{65,97},{97,65},{2,34}... | collective-permute-start | bytes 442376 | tf_op jit(solution)/shard_map/ppermute | solution.py:46
  28.7 10.5 %collective-permute-start.9 = (bf16[256,512]{1,0:T(8,128)(2,1)S(1)}, bf16[256,512]{1,0:T(8,128)(2,1)S(1)}, u32[]{:S(2)}, u32[]{:S(2)}) collective-permute-start(bf16[256,512]{1,0:T(8,128)(2,1)S(1)} %get-tuple-element.43), channel_id=1, source_target_pairs={{0,96},{32,64},{64,32},{96,0},{1,97},{33,65},{65,33},{97,1},{2,98}... | collective-permute-start | bytes 786440 | tf_op jit(solution)/shard_map/ppermute | solution.py:46
  39.3 6.5 %collective-permute-start.10 = (bf16[256,256]{1,0:T(8,128)(2,1)S(1)}, bf16[256,256]{1,0:T(8,128)(2,1)S(1)}, u32[]{:S(2)}, u32[]{:S(2)}) collective-permute-start(bf16[256,256]{1,0:T(8,128)(2,1)S(1)} %far.1), channel_id=1, source_target_pairs={{0,24},{8,16},{16,8},{24,0},{1,25},{9,17},{17,9},{25,1},{2,26},{10... | collective-permute-start | bytes 393224 | tf_op jit(solution)/shard_map/ppermute | solution.py:46
  45.8 4.3 %collective-permute-start.11 = (bf16[128,256]{1,0:T(8,128)(2,1)S(1)}, bf16[128,256]{1,0:T(8,128)(2,1)S(1)}, u32[]{:S(2)}, u32[]{:S(2)}) collective-permute-start(bf16[128,256]{1,0:T(8,128)(2,1)S(1)} %get-tuple-element.46), channel_id=1, source_target_pairs={{0,8},{8,0},{16,24},{24,16},{1,9},{9,1},{17,25},{25,17},{2,10},{10... | collective-permute-start | bytes 196616 | tf_op jit(solution)/shard_map/ppermute | solution.py:46
